TPU v7x, 32 devices: a whole 2x2x4 slice. The times are simulated.
32 devices in a mesh: blk: 8 (over z, x), pair: 4 (over y, core).
Axes of the slice: x: 2, y: 2, z: 4, core: 2. Of those that a mesh axis runs over, the one named last changes fastest.
Arguments:
- records: bfloat16 [8, 1024, 2048], P('blk', 'pair'), may hold values from -100 to 100
- offsets: int32 [2], replicated, may hold values from 1 to 7, as said below
- source_side: int32 [8, 2], P('blk'), may hold values from 0 to 1
Outputs:
- first_side: bfloat16 [8, 2, 32, 128, 128], P('blk', None, 'pair')
- second_side: bfloat16 [8, 2, 32, 128, 128], P('blk', None, 'pair')
Inputs may be any that keep to these rules, and one draw needn't show every extreme that they name: `offsets`: distinct and increasing; the last one is 7.
All inputs are finite; a program needn't handle non-finite values.
Results may differ from a plain program's by a relative error of at most 0.012.
Values may be sent and summed in bfloat16 or wider, within the bound.
No kernel may reach another device: no remote copies, remote signals or barrier semaphores. Data moves between devices by JAX's collectives and lax.ppermute only.
A program may use at most 128 MiB of HBM per device.

v0:
```python
import math

import jax
import jax.numpy as jnp
import numpy as np
from jax import lax
from jax.experimental import pallas as pl
from jax.experimental.pallas import tpu as pltpu
from jax.sharding import PartitionSpec as P


BLOCK_CH = 128
BINS = 128
SAMPLES = 2048
FIRST_BIN = 4
LAGS = 32
HALF_CH = BLOCK_CH // 2
BLOCKS_PER_STEP = 2
DEPTH_CHUNKS = 4
TURNS = ((0, 2), (6, 4), (4, 4), (1, 2), (3, 2), (5, 2), (7, 2), (2, 2))
SEGS_PER_STEP = 8
FLAG_ROWS = 8
SMEM_SPEC = pl.BlockSpec(memory_space=pltpu.SMEM)
VMEM_SPEC = pl.BlockSpec(memory_space=pltpu.VMEM)


def fourier_table():
    sample_index = np.arange(SAMPLES)
    bin_index = FIRST_BIN + np.arange(BINS)
    angles = 2.0 * math.pi / SAMPLES * (sample_index[:, None] * bin_index[None, :] % SAMPLES)
    hann_taper = 0.5 - 0.5 * np.cos(2.0 * math.pi / SAMPLES * sample_index)
    full = np.concatenate(
        (hann_taper[:, None] * np.cos(angles), -hann_taper[:, None] * np.sin(angles)), axis=1
    ).astype(np.float32)
    high = full.astype(jnp.bfloat16)
    low = (full - high.astype(np.float32)).astype(jnp.bfloat16)
    return np.concatenate((high, low), axis=1)


def lag_tables(pairs):
    theta = 2.0 * math.pi / SAMPLES * (FIRST_BIN + np.arange(BINS))
    lag_local = LAGS // pairs
    middle = np.arange(pairs) * lag_local + 0.5 * (lag_local - 1) - LAGS // 2
    away = (np.arange(lag_local // 2) + 0.5)[:, None] * theta
    middle = middle[:, None] * theta
    tables = np.cos(middle), np.sin(middle), np.stack((np.cos(away), np.sin(away), -np.sin(away)))
    return [jnp.asarray(table.astype(np.float32)) for table in tables]


def whiten(records, half_of):
    blocks = records.shape[0] // BLOCK_CH
    step_blocks = min(BLOCKS_PER_STEP, blocks)
    step_rows = step_blocks * BLOCK_CH
    depth = SAMPLES // DEPTH_CHUNKS

    def kernel(records_hbm, table_hbm, mine_ref, other_ref, held, traces, table, trace_sem, table_sem):
        step = pl.program_id(0)
        half = half_of(lax.axis_index("pair"))

        def trace_copy(a):
            part = pl.ds(a * depth, depth)
            source = records_hbm.at[pl.ds(step * step_rows, step_rows), part]
            return pltpu.make_async_copy(source, traces.at[:, part], trace_sem.at[a])

        def table_copy(a):
            part = pl.ds(a * depth, depth)
            return pltpu.make_async_copy(table_hbm.at[part], table.at[part], table_sem.at[a])

        for a in range(DEPTH_CHUNKS):
            trace_copy(a).start()
            pl.when(step == 0)(table_copy(a).start)
        both = jnp.zeros((step_rows, 4 * BINS), jnp.float32)
        for a in range(DEPTH_CHUNKS):
            trace_copy(a).wait()
            pl.when(step == 0)(table_copy(a).wait)
            part = slice(a * depth, (a + 1) * depth)
            both += jnp.dot(traces[:, part], table[part], preferred_element_type=jnp.float32)
        spectrum = both[:, : 2 * BINS] + both[:, 2 * BINS :]
        for block in range(step_blocks):
            part = spectrum[block * BLOCK_CH : (block + 1) * BLOCK_CH]
            real, imag = part[:, :BINS], part[:, BINS:]
            level = jnp.mean(real * real + imag * imag, axis=0, keepdims=True)
            scale = 1.0 / jnp.sqrt(level + 1e-05)
            for index, value in enumerate((real * scale, imag * scale)):
                rounded = value.astype(jnp.bfloat16)
                held[block, 0, index] = rounded[:HALF_CH]
                held[block, 1, index] = rounded[HALF_CH:]
            mine_ref[step * step_blocks + block] = held[block, half]
            other_ref[step * step_blocks + block] = held[block, 1 - half]

    shape = (blocks, 2, HALF_CH, BINS)
    return pl.pallas_call(
        kernel,
        grid=(blocks // step_blocks,),
        in_specs=[pl.BlockSpec(memory_space=pl.ANY)] * 2,
        out_specs=[VMEM_SPEC] * 2,
        out_shape=[pltpu.VMEM(shape, jnp.bfloat16)] * 2,
        scratch_shapes=[
            pltpu.VMEM((step_blocks, 2, 2, HALF_CH, BINS), jnp.bfloat16),
            pltpu.VMEM((step_rows, SAMPLES), jnp.bfloat16),
            pltpu.VMEM((SAMPLES, 4 * BINS), jnp.bfloat16),
            pltpu.SemaphoreType.DMA((DEPTH_CHUNKS,)),
            pltpu.SemaphoreType.DMA((DEPTH_CHUNKS,)),
        ],
        name="whiten",
    )(records, jnp.asarray(fourier_table()))


def group_is_window(group, offset_total):
    return group <= 16 and offset_total == 2


def slot_total(group, offset_total):
    return 2 if group_is_window(group, offset_total) else 2 * offset_total


def slot_pair(row, slot, offset_at, group, offset_total):
    if group_is_window(group, offset_total):
        last = group - 1
        if slot == 0:
            ahead = row + offset_at(0)
            inside = ahead < group
            return jnp.where(inside, 0, 1), jnp.where(inside, 0, 1), jnp.where(inside, ahead, row - last)
        behind = row - offset_at(0)
        inside = behind >= 0
        return jnp.where(inside, 1, 0), jnp.where(inside, 0, 1), jnp.where(inside, behind, row + last)
    side, k = slot // offset_total, slot % offset_total
    return side, k, row - offset_at(k) if side else row + offset_at(k)


def in_vmem(value):
    return pltpu.with_memory_space_constraint(value, pltpu.VMEM)


def part_top(pair, parts):
    top = pair % 2 * HALF_CH
    return top if parts == 2 else top + pair // 2 % 2 * (HALF_CH // 2)


def flag_at(slots, parts):
    return (1 + slots) * 2 * (BLOCK_CH // parts)


def pack(pieces, offsets, source_side, group, turns):
    offset_total = offsets.shape[0]
    slots = slot_total(group, offset_total)
    piece_blocks = pieces[0].shape[0]

    def kernel(offsets_ref, side_ref, *refs):
        piece_refs, out_refs, held = refs[: len(pieces)], refs[len(pieces) : -1], refs[-1]
        own_row, pair = lax.axis_index("blk"), lax.axis_index("pair")
        for turn, piece_ref in enumerate(piece_refs):
            first = (pair ^ turn) * piece_blocks
            for block in range(piece_blocks):
                held[first + block] = piece_ref[block]
        lane = lax.broadcasted_iota(jnp.int32, (FLAG_ROWS, BINS), 1)
        flags = jnp.zeros((FLAG_ROWS, BINS), jnp.float32)
        for k in range(offset_total):
            flags = jnp.where(lane == k, side_ref[0, k].astype(jnp.float32), flags)
        flags = flags.astype(jnp.bfloat16)

        def fill(row, out_ref, parts):
            count = BLOCK_CH // parts
            top = pl.multiple_of(part_top(pair, parts) - part_top(pair, 2), count)
            blocks = [row]
            for slot in range(slots):
                _, _, partner = slot_pair(row, slot, lambda k: offsets_ref[k], group, offset_total)
                blocks.append(jnp.clip(partner, 0, group - 1))
            for index, block in enumerate(blocks):
                for part in range(2):
                    at = (2 * index + part) * count
                    out_ref[at : at + count] = held[block, part, pl.ds(top, count)]
            out_ref[flag_at(slots, parts) :] = flags

        if turns:
            for (turn, parts), out_ref in zip(turns, out_refs):
                fill(own_row ^ turn, out_ref, parts)
        else:

            @pl.loop(0, group)
            def _(row):
                fill(row, out_refs[0].at[row], 2)

    def shape(parts):
        return (flag_at(slots, parts) + FLAG_ROWS, BINS)

    if turns:
        out_shape = [pltpu.VMEM(shape(parts), jnp.bfloat16) for _, parts in turns]
    else:
        out_shape = [jax.ShapeDtypeStruct((group,) + shape(2), jnp.bfloat16)]
    return pl.pallas_call(
        kernel,
        in_specs=[SMEM_SPEC, SMEM_SPEC] + [VMEM_SPEC] * len(pieces),
        out_specs=[VMEM_SPEC] * len(out_shape),
        out_shape=out_shape,
        scratch_shapes=[pltpu.VMEM((group, 2, HALF_CH, BINS), jnp.bfloat16)],
        name="pack",
    )(offsets, source_side, *[in_vmem(piece) for piece in pieces])


def describe_slots(row, duo, offsets_ref, side_ref, far_side, group, offset_total):
    found = []
    for a in range(2):
        side, k, other = 0, 0, 0
        for b in range(slot_total(group, offset_total) // 2):
            here = slot_pair(row, 2 * b + a, lambda j: offsets_ref[j], group, offset_total)
            side, k, other = [jnp.where(duo == b, x, y) for x, y in zip(here, (side, k, other))]
        valid = jnp.logical_and(other >= 0, other < group)
        far = far_side(jnp.clip(other, 0, group - 1), k)
        own_source = jnp.where(side == 0, side_ref[0, k] == 0, far)
        found.append((side, k, valid, own_source))
    return found


def fill_factors(segments, slot_list, duo, pair, tables, left, right):
    cos_mid, sin_mid, away = tables
    span = away.shape[1]
    c_mid, s_mid = cos_mid[pl.ds(pair, 1)], sin_mid[pl.ds(pair, 1)]
    for seg, parts in enumerate(segments):
        count = BLOCK_CH // len(parts)
        for turn, ref in enumerate(parts):
            top = pl.multiple_of(part_top(pair ^ turn, len(parts)), count)

            def put(target, part, block, value):
                rows = pl.ds(block * BLOCK_CH + top, count)
                target[2 * seg + part, rows] = value.astype(jnp.bfloat16)

            real, imag = ref[:count].astype(jnp.float32), ref[count : 2 * count].astype(jnp.float32)
            for m in range(span):
                c, s, minus = [away[a, m : m + 1] for a in range(3)]
                put(left, 0, m, real * c)
                put(left, 1, m, imag * c)
                put(left, 0, span + m, imag * minus)
                put(left, 1, span + m, real * s)
            for a, (_, _, _, own_source) in enumerate(slot_list):
                start = pl.multiple_of((2 * duo + a + 1) * 2 * count, 2 * count)
                real = ref[pl.ds(start, count)].astype(jnp.float32)
                imag = ref[pl.ds(start + count, count)].astype(jnp.float32)
                s = s_mid * jnp.where(own_source, 1.0, -1.0)
                put(right, 0, a, real * c_mid - imag * s)
                put(right, 1, a, imag * c_mid + real * s)


def contract(left, right):
    wide = lambda ref: jnp.concatenate([ref[a] for a in range(ref.shape[0])], axis=1)
    return lax.dot_general(
        wide(left), wide(right), (((1,), (1,)), ((), ())), preferred_element_type=jnp.float32
    )


def lag_values(totals, a, span, normalizer, turned, put):
    columns = slice(a * BLOCK_CH, (a + 1) * BLOCK_CH)

    def rows(at):
        found = [total[at * BLOCK_CH : (at + 1) * BLOCK_CH, columns] for total in totals]
        return sum(found[1:], found[0]) * normalizer

    for m in range(span):
        even, odd = rows(m), rows(span + m)
        for lag, plus in ((span - 1 - m, not turned), (span + m, turned)):
            value = even + odd if plus else even - odd
            put(lag, (value.T if turned else value).astype(jnp.bfloat16))


def factor_scratch(segs, span):
    return [
        pltpu.VMEM((2 * segs, 2 * span * BLOCK_CH, BINS), jnp.bfloat16),
        pltpu.VMEM((2 * segs, 2 * BLOCK_CH, BINS), jnp.bfloat16),
    ]


def correlate_all(mine, theirs, offsets, source_side, group, pairs):
    offset_total = offsets.shape[0]
    slots = slot_total(group, offset_total)
    segs = mine.shape[0]
    steps = segs // SEGS_PER_STEP
    lag_local = LAGS // pairs
    span = lag_local // 2
    normalizer = 1.0 / math.sqrt(segs * BINS)
    total_shape = (2 * span * BLOCK_CH, 2 * BLOCK_CH)

    def kernel(offsets_ref, side_ref, *refs):
        tables, (mine_ref, theirs_ref, flags_ref, first_ref, second_ref, left, right, total) = refs[:3], refs[3:]
        duo, step = pl.program_id(0), pl.program_id(1)
        row, pair = lax.axis_index("blk"), lax.axis_index("pair")
        lane = lax.broadcasted_iota(jnp.int32, (FLAG_ROWS, BINS), 1)

        def far_side(other, k):
            return jnp.max(jnp.where(lane == k, flags_ref[other].astype(jnp.float32), 0.0)) > 0.5

        found = describe_slots(row, duo, offsets_ref, side_ref, far_side, group, offset_total)

        @pl.when(jnp.logical_and(duo == 0, step == 0))
        def _():
            first_ref[...] = jnp.zeros_like(first_ref)
            second_ref[...] = jnp.zeros_like(second_ref)

        segments = [(mine_ref.at[a], theirs_ref.at[a]) for a in range(SEGS_PER_STEP)]
        fill_factors(segments, found, duo, pair, tables, left, right)
        product = contract(left, right)

        @pl.when(step == 0)
        def _():
            total[...] = product

        @pl.when(step > 0)
        def _():
            total[...] += product

        for a, (side, k, valid, own_source) in enumerate(found):
            for a_side, out_ref in enumerate((first_ref, second_ref)):
                for turned in (False, True):
                    here = jnp.logical_and(valid, step == steps - 1)
                    here = jnp.logical_and(here, side == a_side)
                    here = jnp.logical_and(here, own_source != turned)

                    @pl.when(here)
                    def _():
                        def put(lag, value):
                            out_ref[0, k, lag] = value

                        lag_values([total], a, span, normalizer, turned, put)

    out_shape = (1, offset_total, lag_local, BLOCK_CH, BLOCK_CH)
    out_spec = pl.BlockSpec(out_shape, lambda a, b: (0, 0, 0, 0, 0))
    flag_block = flag_at(slots, 2) // FLAG_ROWS
    piece = pl.BlockSpec((SEGS_PER_STEP,) + mine.shape[1:], lambda a, b: (b, 0, 0))
    flags = pl.BlockSpec((segs, FLAG_ROWS, BINS), lambda a, b: (0, flag_block, 0))
    return pl.pallas_call(
        kernel,
        grid=(slots // 2, steps),
        in_specs=[SMEM_SPEC, SMEM_SPEC] + [VMEM_SPEC] * 3 + [piece, piece, flags],
        out_specs=[out_spec] * 2,
        out_shape=[jax.ShapeDtypeStruct(out_shape, jnp.bfloat16)] * 2,
        scratch_shapes=factor_scratch(SEGS_PER_STEP, span) + [pltpu.VMEM(total_shape, jnp.float32)],
        name="correlate",
    )(offsets, source_side, *lag_tables(pairs), mine, theirs, mine)


def correlate_turns(turns, segments, offsets, source_side, group, pairs):
    offset_total = offsets.shape[0]
    slots = slot_total(group, offset_total)
    lag_local = LAGS // pairs
    span = lag_local // 2
    normalizer = 1.0 / math.sqrt(len(turns) * BINS)
    total_shape = (2 * span * BLOCK_CH, 2 * BLOCK_CH)
    out_shape = (1, offset_total, lag_local, BLOCK_CH, BLOCK_CH)
    counts = [len(parts) for parts in segments]

    def kernel(offsets_ref, side_ref, *refs):
        tables, refs = refs[:3], refs[3:]
        held = []
        for count in counts:
            held.append(refs[:count])
            refs = refs[count:]
        first_hbm, second_hbm, left, right, total, result, zeros, sems, zero_sems = refs
        row, pair = lax.axis_index("blk"), lax.axis_index("pair")
        lane = lax.broadcasted_iota(jnp.int32, (FLAG_ROWS, BINS), 1)

        def far_side(other, k):
            flags = jnp.zeros((FLAG_ROWS, BINS), jnp.float32)
            for (turn, _), parts in zip(turns, held):
                piece = parts[0][flag_at(slots, len(parts)) :].astype(jnp.float32)
                flags = jnp.where(row ^ turn == other, piece, flags)
            return jnp.max(jnp.where(lane == k, flags, 0.0)) > 0.5

        found = describe_slots(row, 0, offsets_ref, side_ref, far_side, group, offset_total)

        slabs = []
        for side, out_hbm in enumerate((first_hbm, second_hbm)):
            for k in range(offset_total):
                pair_row = row - offsets_ref[k] if side else row + offsets_ref[k]
                is_pair = jnp.logical_and(pair_row >= 0, pair_row < group)
                copy = pltpu.make_async_copy(zeros, out_hbm.at[0, k], zero_sems.at[side, k])
                slabs.append((jnp.logical_not(is_pair), copy))
        zeros[...] = jnp.zeros_like(zeros)
        for blank, copy in slabs:
            pl.when(blank)(copy.start)

        def copy_to(out_hbm, a, k, lag):
            return pltpu.make_async_copy(result.at[a, lag], out_hbm.at[0, k, lag], sems.at[a, lag])

        @pl.when(jnp.logical_or(found[0][2], found[1][2]))
        def _():
            fill_factors(held, found, 0, pair, tables, left, right)
            total[...] = contract(left, right)

        for a, (side, k, valid, own_source) in enumerate(found):
            for turned in (False, True):

                @pl.when(jnp.logical_and(valid, own_source != turned))
                def _():
                    def put(lag, value):
                        result[a, lag] = value
                        pl.when(side == 0)(copy_to(first_hbm, a, k, lag).start)
                        pl.when(side != 0)(copy_to(second_hbm, a, k, lag).start)

                    lag_values([total], a, span, normalizer, turned, put)

        for a, (side, k, valid, own_source) in enumerate(found):

            @pl.when(valid)
            def _():
                for lag in range(lag_local):
                    copy_to(first_hbm, a, 0, lag).wait()

        for blank, copy in slabs:
            pl.when(blank)(copy.wait)

    any_spec = pl.BlockSpec(memory_space=pl.ANY)
    operands = [in_vmem(part) for parts in segments for part in parts]
    return pl.pallas_call(
        kernel,
        in_specs=[SMEM_SPEC, SMEM_SPEC] + [VMEM_SPEC] * (3 + len(operands)),
        out_specs=[any_spec] * 2,
        out_shape=[jax.ShapeDtypeStruct(out_shape, jnp.bfloat16)] * 2,
        scratch_shapes=factor_scratch(len(turns), span)
        + [
            pltpu.VMEM(total_shape, jnp.float32),
            pltpu.VMEM((2, lag_local, BLOCK_CH, BLOCK_CH), jnp.bfloat16),
            pltpu.VMEM((lag_local, BLOCK_CH, BLOCK_CH), jnp.bfloat16),
            pltpu.SemaphoreType.DMA((2, lag_local)),
            pltpu.SemaphoreType.DMA((2, offset_total)),
        ],
        name="correlate",
    )(offsets, source_side, *lag_tables(pairs), *operands)


def local(records, offsets, source_side):
    group, pairs = lax.axis_size("blk"), lax.axis_size("pair")
    half_of = lambda pair: pair % 2
    assert records.shape[0] == 1

    def swap(value, axis, turn):
        return lax.ppermute(value, axis, [(a, a ^ turn) for a in range(lax.axis_size(axis))])

    mine, other = whiten(records.reshape(records.shape[1], SAMPLES), half_of)
    pieces = [mine]
    for turn in range(1, pairs):
        pieces.append(swap(other if turn % 2 else mine, "pair", turn))
    turns = turns_of(group, pairs)
    packed = pack(pieces, offsets, source_side, group, turns)
    if not turns:
        arrived = lax.all_to_all(packed[0], "blk", split_axis=0, concat_axis=0, tiled=True)
        theirs = swap(arrived, "pair", 1)
        return correlate_all(arrived, theirs, offsets, source_side, group, pairs)
    segments = []
    for (turn, parts), value in zip(turns, packed):
        arrived = swap(value, "blk", turn) if turn else value
        hops = [swap(arrived, "pair", hop) for hop in range(1, parts)]
        segments.append([arrived] + hops)
    return correlate_turns(turns, segments, offsets, source_side, group, pairs)


def turns_of(group, pairs):
    return TURNS if group == len(TURNS) and pairs == 4 else ()


def solution(mesh):
    placed = (P("blk", "pair", None), P(), P("blk", None))

    return jax.shard_map(
        local,
        mesh=mesh,
        in_specs=placed,
        out_specs=(P("blk", None, "pair", None, None), P("blk", None, "pair", None, None)),
        check_vma=False,
    )
```

profile of v0, /device:TPU:0, one launch (start us, length us, event | category | flops | bytes accessed | tf_op | source)
XLA Modules:
  0.0 40.2 jit_solution(11536995702129323785)
XLA Ops:
  0.6 2.9 %whiten.1 = (bf16[2,2,64,128]{3,2,1,0:T(8,128)(2,1)S(1)}, bf16[2,2,64,128]{3,2,1,0:T(8,128)(2,1)S(1)}) custom-call(bf16[256,2048]{1,0:T(8,128)(2,1)} %bitcast.1, bf16[2048,512]{1,0:T(8,128)(2,1)} %constant.8.clone.table_hbm), custom_call_target="tpu_custom_call" | custom-call | tf_op jit(solution)/shard_map/whiten/pallas_call | solution.py:92
  3.5 3.1 %collective-permute-start.1 = (bf16[2,2,64,128]{3,2,1,0:T(8,128)(2,1)S(1)}, bf16[2,2,64,128]{3,2,1,0:T(8,128)(2,1)S(1)}, u32[]{:S(2)}, u32[]{:S(2)}) collective-permute-start(bf16[2,2,64,128]{3,2,1,0:T(8,128)(2,1)S(1)} %get-tuple-element.12.refs_0_), channel_id=1, source_target_pairs={{0,2},{1,3},{2,0},{3,1},{4,6},{5,7},{6,4},{7,5},{8,10},{9,11},{10,... | collective-permute-start | bytes 196616 | tf_op jit(solution)/shard_map/ppermute | solution.py:435
  6.8 2.1 %collective-permute-done.1.refs_2_ = bf16[2,2,64,128]{3,2,1,0:T(8,128)(2,1)S(1)} collective-permute-done((bf16[2,2,64,128]{3,2,1,0:T(8,128)(2,1)S(1)}, bf16[2,2,64,128]{3,2,1,0:T(8,128)(2,1)S(1)}, u32[]{:S(2)}, u32[]{:S(2)}) %collective-permute-start.1) | collective-permute-done | bytes 65568 | tf_op jit(solution)/shard_map/ppermute | solution.py:435
  8.9 1.9 %collective-permute-done.2.refs_3_ = bf16[2,2,64,128]{3,2,1,0:T(8,128)(2,1)S(1)} collective-permute-done((bf16[2,2,64,128]{3,2,1,0:T(8,128)(2,1)S(1)}, bf16[2,2,64,128]{3,2,1,0:T(8,128)(2,1)S(1)}, u32[]{:S(2)}, u32[]{:S(2)}) %collective-permute-start.2) | collective-permute-done | bytes 65568 | tf_op jit(solution)/shard_map/ppermute | solution.py:435
  10.7 0.8 %pack.1 = (bf16[392,128]{1,0:T(8,128)(2,1)S(1)}, bf16[200,128]{1,0:T(8,128)(2,1)S(1)}, bf16[200,128]{1,0:T(8,128)(2,1)S(1)}, bf16[392,128]{1,0:T(8,128)(2,1)S(1)...) custom-call(s32[2]{0:T(128)} %offsets_ref.3, ...), custom_call_target="tpu_custom_call" | custom-call | tf_op jit(solution)/shard_map/pack/pallas_call | solution.py:191
  11.5 1.6 %collective-permute-start.12 = (bf16[392,128]{1,0:T(8,128)(2,1)S(1)}, bf16[392,128]{1,0:T(8,128)(2,1)S(1)}, u32[]{:S(2)}, u32[]{:S(2)}) collective-permute-start(bf16[392,128]{1,0:T(8,128)(2,1)S(1)} %get-tuple-element.17), channel_id=1, source_target_pairs={{0,4},{4,0},{8,12},{12,8},{16,20},{20,16},{24,28},{28,24},{1,5},{5... | collective-permute-start | bytes 301064 | tf_op jit(solution)/shard_map/ppermute | solution.py:435
  13.1 3.6 %collective-permute-start.4 = (bf16[200,128]{1,0:T(8,128)(2,1)S(1)}, bf16[200,128]{1,0:T(8,128)(2,1)S(1)}, u32[]{:S(2)}, u32[]{:S(2)}) collective-permute-start(bf16[200,128]{1,0:T(8,128)(2,1)S(1)} %get-tuple-element.15), channel_id=1, source_target_pairs={{0,24},{4,28},{8,16},{12,20},{16,8},{20,12},{24,0},{28,4},{1,25},{... | collective-permute-start | bytes 153608 | tf_op jit(solution)/shard_map/ppermute | solution.py:435
  16.7 0.7 %collective-permute-start.14 = (bf16[392,128]{1,0:T(8,128)(2,1)S(1)}, bf16[392,128]{1,0:T(8,128)(2,1)S(1)}, u32[]{:S(2)}, u32[]{:S(2)}) collective-permute-start(bf16[392,128]{1,0:T(8,128)(2,1)S(1)} %get-tuple-element.18), channel_id=1, source_target_pairs={{0,12},{4,8},{8,4},{12,0},{16,28},{20,24},{24,20},{28,16},{1,13},{... | collective-permute-start | bytes 301064 | tf_op jit(solution)/shard_map/ppermute | solution.py:435
  17.4 2.6 %collective-permute-start.16 = (bf16[392,128]{1,0:T(8,128)(2,1)S(1)}, bf16[392,128]{1,0:T(8,128)(2,1)S(1)}, u32[]{:S(2)}, u32[]{:S(2)}) collective-permute-start(bf16[392,128]{1,0:T(8,128)(2,1)S(1)} %get-tuple-element.19), channel_id=1, source_target_pairs={{0,20},{4,16},{8,28},{12,24},{16,4},{20,0},{24,12},{28,8},{1,21},{... | collective-permute-start | bytes 301064 | tf_op jit(solution)/shard_map/ppermute | solution.py:435
  20.1 3.1 %collective-permute-start.18 = (bf16[392,128]{1,0:T(8,128)(2,1)S(1)}, bf16[392,128]{1,0:T(8,128)(2,1)S(1)}, u32[]{:S(2)}, u32[]{:S(2)}) collective-permute-start(bf16[392,128]{1,0:T(8,128)(2,1)S(1)} %get-tuple-element.20), channel_id=1, source_target_pairs={{0,28},{4,24},{8,20},{12,16},{16,12},{20,8},{24,4},{28,0},{1,29},{... | collective-permute-start | bytes 301064 | tf_op jit(solution)/shard_map/ppermute | solution.py:435
  23.4 0.7 %collective-permute-done.14.refs_15_ = bf16[392,128]{1,0:T(8,128)(2,1)S(1)} collective-permute-done((bf16[392,128]{1,0:T(8,128)(2,1)S(1)}, bf16[392,128]{1,0:T(8,128)(2,1)S(1)}, u32[]{:S(2)}, u32[]{:S(2)}) %collective-permute-start.14) | collective-permute-done | bytes 100384 | tf_op jit(solution)/shard_map/ppermute | solution.py:435
  24.0 1.3 %collective-permute-start.7 = (bf16[200,128]{1,0:T(8,128)(2,1)S(1)}, bf16[200,128]{1,0:T(8,128)(2,1)S(1)}, u32[]{:S(2)}, u32[]{:S(2)}) collective-permute-start(bf16[200,128]{1,0:T(8,128)(2,1)S(1)} %collective-permute-done.4.refs_5_), channel_id=1, source_target_pairs={{0,3},{1,2},{2,1},{3,0},{4,7},{5,6},{6,5},{7,4},{8,11},{9,10},{10,... | collective-permute-start | bytes 153608 | tf_op jit(solution)/shard_map/ppermute | solution.py:435
  25.4 2.4 %collective-permute-done.16.refs_17_ = bf16[392,128]{1,0:T(8,128)(2,1)S(1)} collective-permute-done((bf16[392,128]{1,0:T(8,128)(2,1)S(1)}, bf16[392,128]{1,0:T(8,128)(2,1)S(1)}, u32[]{:S(2)}, u32[]{:S(2)}) %collective-permute-start.16) | collective-permute-done | bytes 100384 | tf_op jit(solution)/shard_map/ppermute | solution.py:435
  27.8 1.3 %collective-permute-done.18.refs_19_ = bf16[392,128]{1,0:T(8,128)(2,1)S(1)} collective-permute-done((bf16[392,128]{1,0:T(8,128)(2,1)S(1)}, bf16[392,128]{1,0:T(8,128)(2,1)S(1)}, u32[]{:S(2)}, u32[]{:S(2)}) %collective-permute-start.18) | collective-permute-done | bytes 100384 | tf_op jit(solution)/shard_map/ppermute | solution.py:435
  29.3 1.3 %collective-permute-start.11 = (bf16[200,128]{1,0:T(8,128)(2,1)S(1)}, bf16[200,128]{1,0:T(8,128)(2,1)S(1)}, u32[]{:S(2)}, u32[]{:S(2)}) collective-permute-start(bf16[200,128]{1,0:T(8,128)(2,1)S(1)} %collective-permute-done.8.refs_9_), channel_id=1, source_target_pairs={{0,3},{1,2},{2,1},{3,0},{4,7},{5,6},{6,5},{7,4},{8,11},{9,10},{10,... | collective-permute-start | bytes 153608 | tf_op jit(solution)/shard_map/ppermute | solution.py:435
  30.6 0.6 %collective-permute-start.10 = (bf16[200,128]{1,0:T(8,128)(2,1)S(1)}, bf16[200,128]{1,0:T(8,128)(2,1)S(1)}, u32[]{:S(2)}, u32[]{:S(2)}) collective-permute-start(bf16[200,128]{1,0:T(8,128)(2,1)S(1)} %collective-permute-done.8.refs_9_), channel_id=1, source_target_pairs={{0,2},{1,3},{2,0},{3,1},{4,6},{5,7},{6,4},{7,5},{8,10},{9,11},{10,... | collective-permute-start | bytes 153608 | tf_op jit(solution)/shard_map/ppermute | solution.py:435
  31.3 0.7 %collective-permute-done.6.refs_7_ = bf16[200,128]{1,0:T(8,128)(2,1)S(1)} collective-permute-done((bf16[200,128]{1,0:T(8,128)(2,1)S(1)}, bf16[200,128]{1,0:T(8,128)(2,1)S(1)}, u32[]{:S(2)}, u32[]{:S(2)}) %collective-permute-start.6) | collective-permute-done | bytes 51232 | tf_op jit(solution)/shard_map/ppermute | solution.py:435
  31.9 0.5 %collective-permute-start.15 = (bf16[392,128]{1,0:T(8,128)(2,1)S(1)}, bf16[392,128]{1,0:T(8,128)(2,1)S(1)}, u32[]{:S(2)}, u32[]{:S(2)}) collective-permute-start(bf16[392,128]{1,0:T(8,128)(2,1)S(1)} %collective-permute-done.14.refs_15_), channel_id=1, source_target_pairs={{0,1},{1,0},{2,3},{3,2},{4,5},{5,4},{6,7},{7,6},{8,9},{9,8},{10,11... | collective-permute-start | bytes 301064 | tf_op jit(solution)/shard_map/ppermute | solution.py:435
  32.4 0.5 %collective-permute-done.11.refs_12_ = bf16[200,128]{1,0:T(8,128)(2,1)S(1)} collective-permute-done((bf16[200,128]{1,0:T(8,128)(2,1)S(1)}, bf16[200,128]{1,0:T(8,128)(2,1)S(1)}, u32[]{:S(2)}, u32[]{:S(2)}) %collective-permute-start.11) | collective-permute-done | bytes 51232 | tf_op jit(solution)/shard_map/ppermute | solution.py:435
  32.9 0.5 %collective-permute-start.17 = (bf16[392,128]{1,0:T(8,128)(2,1)S(1)}, bf16[392,128]{1,0:T(8,128)(2,1)S(1)}, u32[]{:S(2)}, u32[]{:S(2)}) collective-permute-start(bf16[392,128]{1,0:T(8,128)(2,1)S(1)} %collective-permute-done.16.refs_17_), channel_id=1, source_target_pairs={{0,1},{1,0},{2,3},{3,2},{4,5},{5,4},{6,7},{7,6},{8,9},{9,8},{10,11... | collective-permute-start | bytes 301064 | tf_op jit(solution)/shard_map/ppermute | solution.py:435
  33.4 1.4 %collective-permute-done.10.refs_11_ = bf16[200,128]{1,0:T(8,128)(2,1)S(1)} collective-permute-done((bf16[200,128]{1,0:T(8,128)(2,1)S(1)}, bf16[200,128]{1,0:T(8,128)(2,1)S(1)}, u32[]{:S(2)}, u32[]{:S(2)}) %collective-permute-start.10) | collective-permute-done | bytes 51232 | tf_op jit(solution)/shard_map/ppermute | solution.py:435
  34.7 0.5 %collective-permute-start.21 = (bf16[392,128]{1,0:T(8,128)(2,1)S(1)}, bf16[392,128]{1,0:T(8,128)(2,1)S(1)}, u32[]{:S(2)}, u32[]{:S(2)}) collective-permute-start(bf16[392,128]{1,0:T(8,128)(2,1)S(1)} %collective-permute-done.20.refs_21_), channel_id=1, source_target_pairs={{0,1},{1,0},{2,3},{3,2},{4,5},{5,4},{6,7},{7,6},{8,9},{9,8},{10,11... | collective-permute-start | bytes 301064 | tf_op jit(solution)/shard_map/ppermute | solution.py:435
  35.3 0.8 %collective-permute-done.19.refs_20_ = bf16[392,128]{1,0:T(8,128)(2,1)S(1)} collective-permute-done((bf16[392,128]{1,0:T(8,128)(2,1)S(1)}, bf16[392,128]{1,0:T(8,128)(2,1)S(1)}, u32[]{:S(2)}, u32[]{:S(2)}) %collective-permute-start.19) | collective-permute-done | bytes 100384 | tf_op jit(solution)/shard_map/ppermute | solution.py:435
  36.2 4.0 %correlate.1 = (bf16[1,2,8,128,128]{4,3,2,1,0:T(8,128)(2,1)}, bf16[1,2,8,128,128]{4,3,2,1,0:T(8,128)(2,1)}) custom-call(s32[2]{0:T(128)} %offsets_ref.3, s32[1,2]{1,0:T(1,128)} %side_ref.3, f32[4,128]{1,0:T(4,128)} %constant.9.clone.refs_0_, f32[4,128]{1,0:T(4,128)} %constant.10.clone.refs_1_, f32[3,4,128]{2,1,0:T(4,128)} %constant.11.clone.refs_2_, ...), custom_call_target="tpu_custom_call" | custom-call | tf_op jit(solution)/shard_map/correlate/pallas_call | solution.py:412
  (23 shorter events, 0.8 us)
Async XLA Ops:
  3.5 5.3 %collective-permute-start.1 = (bf16[2,2,64,128]{3,2,1,0:T(8,128)(2,1)S(1)}, bf16[2,2,64,128]{3,2,1,0:T(8,128)(2,1)S(1)}, u32[]{:S(2)}, u32[]{:S(2)}) collective-permute-start(bf16[2,2,64,128]{3,2,1,0:T(8,128)(2,1)S(1)} %get-tuple-element.12.refs_0_), channel_id=1, source_target_pairs={{0,2},{1,3},{2,0},{3,1},{4,6},{5,7},{6,4},{7,5},{8,10},{9,11},{10,... | collective-permute-start | bytes 196616 | tf_op jit(solution)/shard_map/ppermute | solution.py:435
  6.6 4.1 %collective-permute-start.2 = (bf16[2,2,64,128]{3,2,1,0:T(8,128)(2,1)S(1)}, bf16[2,2,64,128]{3,2,1,0:T(8,128)(2,1)S(1)}, u32[]{:S(2)}, u32[]{:S(2)}) collective-permute-start(bf16[2,2,64,128]{3,2,1,0:T(8,128)(2,1)S(1)} %get-tuple-element.13), channel_id=1, source_target_pairs={{0,3},{1,2},{2,1},{3,0},{4,7},{5,6},{6,5},{7,4},{8,11},{9,10},{10,... | collective-permute-start | bytes 196616 | tf_op jit(solution)/shard_map/ppermute | solution.py:435
  6.6 4.1 %collective-permute-start = (bf16[2,2,64,128]{3,2,1,0:T(8,128)(2,1)S(1)}, bf16[2,2,64,128]{3,2,1,0:T(8,128)(2,1)S(1)}, u32[]{:S(2)}, u32[]{:S(2)}) collective-permute-start(bf16[2,2,64,128]{3,2,1,0:T(8,128)(2,1)S(1)} %get-tuple-element.13), channel_id=1, source_target_pairs={{0,1},{1,0},{2,3},{3,2},{4,5},{5,4},{6,7},{7,6},{8,9},{9,8},{10,11... | collective-permute-start | bytes 196616 | tf_op jit(solution)/shard_map/ppermute | solution.py:435
  11.5 11.9 %collective-permute-start.12 = (bf16[392,128]{1,0:T(8,128)(2,1)S(1)}, bf16[392,128]{1,0:T(8,128)(2,1)S(1)}, u32[]{:S(2)}, u32[]{:S(2)}) collective-permute-start(bf16[392,128]{1,0:T(8,128)(2,1)S(1)} %get-tuple-element.17), channel_id=1, source_target_pairs={{0,4},{4,0},{8,12},{12,8},{16,20},{20,16},{24,28},{28,24},{1,5},{5... | collective-permute-start | bytes 301064 | tf_op jit(solution)/shard_map/ppermute | solution.py:435
  13.1 7.0 %collective-permute-start.4 = (bf16[200,128]{1,0:T(8,128)(2,1)S(1)}, bf16[200,128]{1,0:T(8,128)(2,1)S(1)}, u32[]{:S(2)}, u32[]{:S(2)}) collective-permute-start(bf16[200,128]{1,0:T(8,128)(2,1)S(1)} %get-tuple-element.15), channel_id=1, source_target_pairs={{0,24},{4,28},{8,16},{12,20},{16,8},{20,12},{24,0},{28,4},{1,25},{... | collective-permute-start | bytes 153608 | tf_op jit(solution)/shard_map/ppermute | solution.py:435
  16.7 6.7 %collective-permute-start.8 = (bf16[200,128]{1,0:T(8,128)(2,1)S(1)}, bf16[200,128]{1,0:T(8,128)(2,1)S(1)}, u32[]{:S(2)}, u32[]{:S(2)}) collective-permute-start(bf16[200,128]{1,0:T(8,128)(2,1)S(1)} %get-tuple-element.16), channel_id=1, source_target_pairs={{0,16},{4,20},{8,24},{12,28},{16,0},{20,4},{24,8},{28,12},{1,17},{... | collective-permute-start | bytes 153608 | tf_op jit(solution)/shard_map/ppermute | solution.py:435
  16.7 7.3 %collective-permute-start.14 = (bf16[392,128]{1,0:T(8,128)(2,1)S(1)}, bf16[392,128]{1,0:T(8,128)(2,1)S(1)}, u32[]{:S(2)}, u32[]{:S(2)}) collective-permute-start(bf16[392,128]{1,0:T(8,128)(2,1)S(1)} %get-tuple-element.18), channel_id=1, source_target_pairs={{0,12},{4,8},{8,4},{12,0},{16,28},{20,24},{24,20},{28,16},{1,13},{... | collective-permute-start | bytes 301064 | tf_op jit(solution)/shard_map/ppermute | solution.py:435
  17.4 10.4 %collective-permute-start.16 = (bf16[392,128]{1,0:T(8,128)(2,1)S(1)}, bf16[392,128]{1,0:T(8,128)(2,1)S(1)}, u32[]{:S(2)}, u32[]{:S(2)}) collective-permute-start(bf16[392,128]{1,0:T(8,128)(2,1)S(1)} %get-tuple-element.19), channel_id=1, source_target_pairs={{0,20},{4,16},{8,28},{12,24},{16,4},{20,0},{24,12},{28,8},{1,21},{... | collective-permute-start | bytes 301064 | tf_op jit(solution)/shard_map/ppermute | solution.py:435
  20.1 9.0 %collective-permute-start.18 = (bf16[392,128]{1,0:T(8,128)(2,1)S(1)}, bf16[392,128]{1,0:T(8,128)(2,1)S(1)}, u32[]{:S(2)}, u32[]{:S(2)}) collective-permute-start(bf16[392,128]{1,0:T(8,128)(2,1)S(1)} %get-tuple-element.20), channel_id=1, source_target_pairs={{0,28},{4,24},{8,20},{12,16},{16,12},{20,8},{24,4},{28,0},{1,29},{... | collective-permute-start | bytes 301064 | tf_op jit(solution)/shard_map/ppermute | solution.py:435
  23.4 5.9 %collective-permute-start.20 = (bf16[392,128]{1,0:T(8,128)(2,1)S(1)}, bf16[392,128]{1,0:T(8,128)(2,1)S(1)}, u32[]{:S(2)}, u32[]{:S(2)}) collective-permute-start(bf16[392,128]{1,0:T(8,128)(2,1)S(1)} %get-tuple-element.21), channel_id=1, source_target_pairs={{0,8},{4,12},{8,0},{12,4},{16,24},{20,28},{24,16},{28,20},{1,9},{5... | collective-permute-start | bytes 301064 | tf_op jit(solution)/shard_map/ppermute | solution.py:435
  23.4 7.3 %collective-permute-start.3 = (bf16[392,128]{1,0:T(8,128)(2,1)S(1)}, bf16[392,128]{1,0:T(8,128)(2,1)S(1)}, u32[]{:S(2)}, u32[]{:S(2)}) collective-permute-start(bf16[392,128]{1,0:T(8,128)(2,1)S(1)} %get-tuple-element.14.refs_3_), channel_id=1, source_target_pairs={{0,1},{1,0},{2,3},{3,2},{4,5},{5,4},{6,7},{7,6},{8,9},{9,8},{10,11... | collective-permute-start | bytes 301064 | tf_op jit(solution)/shard_map/ppermute | solution.py:435
  24.0 7.2 %collective-permute-start.7 = (bf16[200,128]{1,0:T(8,128)(2,1)S(1)}, bf16[200,128]{1,0:T(8,128)(2,1)S(1)}, u32[]{:S(2)}, u32[]{:S(2)}) collective-permute-start(bf16[200,128]{1,0:T(8,128)(2,1)S(1)} %collective-permute-done.4.refs_5_), channel_id=1, source_target_pairs={{0,3},{1,2},{2,1},{3,0},{4,7},{5,6},{6,5},{7,4},{8,11},{9,10},{10,... | collective-permute-start | bytes 153608 | tf_op jit(solution)/shard_map/ppermute | solution.py:435
  27.8 4.1 %collective-permute-start.6 = (bf16[200,128]{1,0:T(8,128)(2,1)S(1)}, bf16[200,128]{1,0:T(8,128)(2,1)S(1)}, u32[]{:S(2)}, u32[]{:S(2)}) collective-permute-start(bf16[200,128]{1,0:T(8,128)(2,1)S(1)} %collective-permute-done.4.refs_5_), channel_id=1, source_target_pairs={{0,2},{1,3},{2,0},{3,1},{4,6},{5,7},{6,4},{7,5},{8,10},{9,11},{10,... | collective-permute-start | bytes 153608 | tf_op jit(solution)/shard_map/ppermute | solution.py:435
  29.1 2.8 %collective-permute-start.5 = (bf16[200,128]{1,0:T(8,128)(2,1)S(1)}, bf16[200,128]{1,0:T(8,128)(2,1)S(1)}, u32[]{:S(2)}, u32[]{:S(2)}) collective-permute-start(bf16[200,128]{1,0:T(8,128)(2,1)S(1)} %collective-permute-done.4.refs_5_), channel_id=1, source_target_pairs={{0,1},{1,0},{2,3},{3,2},{4,5},{5,4},{6,7},{7,6},{8,9},{9,8},{10,11... | collective-permute-start | bytes 153608 | tf_op jit(solution)/shard_map/ppermute | solution.py:435
  29.3 3.6 %collective-permute-start.11 = (bf16[200,128]{1,0:T(8,128)(2,1)S(1)}, bf16[200,128]{1,0:T(8,128)(2,1)S(1)}, u32[]{:S(2)}, u32[]{:S(2)}) collective-permute-start(bf16[200,128]{1,0:T(8,128)(2,1)S(1)} %collective-permute-done.8.refs_9_), channel_id=1, source_target_pairs={{0,3},{1,2},{2,1},{3,0},{4,7},{5,6},{6,5},{7,4},{8,11},{9,10},{10,... | collective-permute-start | bytes 153608 | tf_op jit(solution)/shard_map/ppermute | solution.py:435
  30.6 4.1 %collective-permute-start.10 = (bf16[200,128]{1,0:T(8,128)(2,1)S(1)}, bf16[200,128]{1,0:T(8,128)(2,1)S(1)}, u32[]{:S(2)}, u32[]{:S(2)}) collective-permute-start(bf16[200,128]{1,0:T(8,128)(2,1)S(1)} %collective-permute-done.8.refs_9_), channel_id=1, source_target_pairs={{0,2},{1,3},{2,0},{3,1},{4,6},{5,7},{6,4},{7,5},{8,10},{9,11},{10,... | collective-permute-start | bytes 153608 | tf_op jit(solution)/shard_map/ppermute | solution.py:435
  31.2 3.5 %collective-permute-start.9 = (bf16[200,128]{1,0:T(8,128)(2,1)S(1)}, bf16[200,128]{1,0:T(8,128)(2,1)S(1)}, u32[]{:S(2)}, u32[]{:S(2)}) collective-permute-start(bf16[200,128]{1,0:T(8,128)(2,1)S(1)} %collective-permute-done.8.refs_9_), channel_id=1, source_target_pairs={{0,1},{1,0},{2,3},{3,2},{4,5},{5,4},{6,7},{7,6},{8,9},{9,8},{10,11... | collective-permute-start | bytes 153608 | tf_op jit(solution)/shard_map/ppermute | solution.py:435
  31.9 3.3 %collective-permute-start.13 = (bf16[392,128]{1,0:T(8,128)(2,1)S(1)}, bf16[392,128]{1,0:T(8,128)(2,1)S(1)}, u32[]{:S(2)}, u32[]{:S(2)}) collective-permute-start(bf16[392,128]{1,0:T(8,128)(2,1)S(1)} %collective-permute-done.12.refs_13_), channel_id=1, source_target_pairs={{0,1},{1,0},{2,3},{3,2},{4,5},{5,4},{6,7},{7,6},{8,9},{9,8},{10,11... | collective-permute-start | bytes 301064 | tf_op jit(solution)/shard_map/ppermute | solution.py:435
  31.9 3.3 %collective-permute-start.15 = (bf16[392,128]{1,0:T(8,128)(2,1)S(1)}, bf16[392,128]{1,0:T(8,128)(2,1)S(1)}, u32[]{:S(2)}, u32[]{:S(2)}) collective-permute-start(bf16[392,128]{1,0:T(8,128)(2,1)S(1)} %collective-permute-done.14.refs_15_), channel_id=1, source_target_pairs={{0,1},{1,0},{2,3},{3,2},{4,5},{5,4},{6,7},{7,6},{8,9},{9,8},{10,11... | collective-permute-start | bytes 301064 | tf_op jit(solution)/shard_map/ppermute | solution.py:435
  32.9 2.4 %collective-permute-start.17 = (bf16[392,128]{1,0:T(8,128)(2,1)S(1)}, bf16[392,128]{1,0:T(8,128)(2,1)S(1)}, u32[]{:S(2)}, u32[]{:S(2)}) collective-permute-start(bf16[392,128]{1,0:T(8,128)(2,1)S(1)} %collective-permute-done.16.refs_17_), channel_id=1, source_target_pairs={{0,1},{1,0},{2,3},{3,2},{4,5},{5,4},{6,7},{7,6},{8,9},{9,8},{10,11... | collective-permute-start | bytes 301064 | tf_op jit(solution)/shard_map/ppermute | solution.py:435
  34.7 1.3 %collective-permute-start.19 = (bf16[392,128]{1,0:T(8,128)(2,1)S(1)}, bf16[392,128]{1,0:T(8,128)(2,1)S(1)}, u32[]{:S(2)}, u32[]{:S(2)}) collective-permute-start(bf16[392,128]{1,0:T(8,128)(2,1)S(1)} %collective-permute-done.18.refs_19_), channel_id=1, source_target_pairs={{0,1},{1,0},{2,3},{3,2},{4,5},{5,4},{6,7},{7,6},{8,9},{9,8},{10,11... | collective-permute-start | bytes 301064 | tf_op jit(solution)/shard_map/ppermute | solution.py:435
  34.7 1.5 %collective-permute-start.21 = (bf16[392,128]{1,0:T(8,128)(2,1)S(1)}, bf16[392,128]{1,0:T(8,128)(2,1)S(1)}, u32[]{:S(2)}, u32[]{:S(2)}) collective-permute-start(bf16[392,128]{1,0:T(8,128)(2,1)S(1)} %collective-permute-done.20.refs_21_), channel_id=1, source_target_pairs={{0,1},{1,0},{2,3},{3,2},{4,5},{5,4},{6,7},{7,6},{8,9},{9,8},{10,11... | collective-permute-start | bytes 301064 | tf_op jit(solution)/shard_map/ppermute | solution.py:435
where the time goes:
time: 40.4 us; the launch traced here: 40.2 us
  starting transfers between devices  19.6 us (49%)
  waiting for transfers between devices  12.2 us (30%)
  Pallas kernels  7.67 us (19%)
  between operations  0.68 us (2%)
    ppermute x22, starting transfers between devices, swap(): lax.ppermute(value, axis, [(a, a ^ turn) for a in range(lax.axis_size(axi...  19.6 us
    ppermute x22, waiting for transfers between devices, swap(): lax.ppermute(value, axis, [(a, a ^ turn) for a in range(lax.axis_size(axi...  12.2 us
    pallas_call x1, Pallas kernels, correlate_turns(): pl.pallas_call(kernel, in_specs=[SMEM_SPEC, SMEM_SPEC] + [VMEM_SPEC] * (3...  4 us
    pallas_call x1, Pallas kernels, whiten(): pl.pallas_call(kernel, grid=(blocks // step_blocks,), in_specs=[pl.BlockS...  2.91 us
  transfers between devices with their start and end apart: 22, of which 12 were waited for; matrix products, arithmetic and copies ran while one was open for 0% of the time, Pallas kernels for 0%

commit v1 on v0

--- a/solution.py
+++ b/solution.py
@@ -16,11 +16,10 @@
 LAGS = 32
 HALF_CH = BLOCK_CH // 2
 BLOCKS_PER_STEP = 2
-DEPTH_CHUNKS = 4
+DEPTH_CHUNKS = 2
 TURNS = ((0, 2), (6, 4), (4, 4), (1, 2), (3, 2), (5, 2), (7, 2), (2, 2))
 SEGS_PER_STEP = 8
 FLAG_ROWS = 8
-SMEM_SPEC = pl.BlockSpec(memory_space=pltpu.SMEM)
 VMEM_SPEC = pl.BlockSpec(memory_space=pltpu.VMEM)
 
 
@@ -37,23 +36,25 @@
     return np.concatenate((high, low), axis=1)
 
 
-def lag_tables(pairs):
+def lag_tables(pairs, normalizer):
     theta = 2.0 * math.pi / SAMPLES * (FIRST_BIN + np.arange(BINS))
     lag_local = LAGS // pairs
     middle = np.arange(pairs) * lag_local + 0.5 * (lag_local - 1) - LAGS // 2
     away = (np.arange(lag_local // 2) + 0.5)[:, None] * theta
     middle = middle[:, None] * theta
-    tables = np.cos(middle), np.sin(middle), np.stack((np.cos(away), np.sin(away), -np.sin(away)))
+    tables = normalizer * np.cos(middle), normalizer * np.sin(middle), np.stack((np.cos(away), np.sin(away), -np.sin(away)))
     return [jnp.asarray(table.astype(np.float32)) for table in tables]
 
 
-def whiten(records, half_of):
+def whiten(records, offsets, source_side, half_of):
+    offset_total = offsets.shape[0]
     blocks = records.shape[0] // BLOCK_CH
     step_blocks = min(BLOCKS_PER_STEP, blocks)
     step_rows = step_blocks * BLOCK_CH
     depth = SAMPLES // DEPTH_CHUNKS
 
-    def kernel(records_hbm, table_hbm, mine_ref, other_ref, held, traces, table, trace_sem, table_sem):
+    def kernel(offsets_hbm, side_hbm, records_hbm, table_hbm, mine_ref, other_ref, info_ref, *scratch):
+        held, traces, table, offsets_ref, side_ref, trace_sem, table_sem, small_sem = scratch
         step = pl.program_id(0)
         half = half_of(lax.axis_index("pair"))
 
@@ -69,6 +70,20 @@
         for a in range(DEPTH_CHUNKS):
             trace_copy(a).start()
             pl.when(step == 0)(table_copy(a).start)
+        small = (
+            pltpu.make_async_copy(offsets_hbm, offsets_ref, small_sem.at[0]),
+            pltpu.make_async_copy(side_hbm, side_ref, small_sem.at[1]),
+        )
+        for copy in small:
+            copy.start()
+        for copy in small:
+            copy.wait()
+        lane = lax.broadcasted_iota(jnp.int32, (FLAG_ROWS, BINS), 1)
+        info = jnp.zeros((FLAG_ROWS, BINS), jnp.int32)
+        for k in range(offset_total):
+            info = jnp.where(lane == k, side_ref[0, k], info)
+            info = jnp.where(lane == FLAG_ROWS + k, offsets_ref[k], info)
+        info_ref[...] = info.astype(jnp.float32)
         both = jnp.zeros((step_rows, 4 * BINS), jnp.float32)
         for a in range(DEPTH_CHUNKS):
             trace_copy(a).wait()
@@ -92,18 +107,21 @@
     return pl.pallas_call(
         kernel,
         grid=(blocks // step_blocks,),
-        in_specs=[pl.BlockSpec(memory_space=pl.ANY)] * 2,
-        out_specs=[VMEM_SPEC] * 2,
-        out_shape=[pltpu.VMEM(shape, jnp.bfloat16)] * 2,
+        in_specs=[pl.BlockSpec(memory_space=pl.ANY)] * 4,
+        out_specs=[VMEM_SPEC] * 3,
+        out_shape=[pltpu.VMEM(shape, jnp.bfloat16)] * 2 + [pltpu.VMEM((FLAG_ROWS, BINS), jnp.float32)],
         scratch_shapes=[
             pltpu.VMEM((step_blocks, 2, 2, HALF_CH, BINS), jnp.bfloat16),
             pltpu.VMEM((step_rows, SAMPLES), jnp.bfloat16),
             pltpu.VMEM((SAMPLES, 4 * BINS), jnp.bfloat16),
+            pltpu.SMEM(offsets.shape, jnp.int32),
+            pltpu.SMEM(source_side.shape, jnp.int32),
             pltpu.SemaphoreType.DMA((DEPTH_CHUNKS,)),
             pltpu.SemaphoreType.DMA((DEPTH_CHUNKS,)),
+            pltpu.SemaphoreType.DMA((2,)),
         ],
         name="whiten",
-    )(records, jnp.asarray(fourier_table()))
+    )(offsets, source_side, records, jnp.asarray(fourier_table()))
 
 
 def group_is_window(group, offset_total):
@@ -141,30 +159,32 @@
     return (1 + slots) * 2 * (BLOCK_CH // parts)
 
 
-def pack(pieces, offsets, source_side, group, turns):
-    offset_total = offsets.shape[0]
+def read_info(info_ref, offset_total):
+    lane = lax.broadcasted_iota(jnp.int32, (FLAG_ROWS, BINS), 1)
+    at = lambda index: jnp.max(jnp.where(lane == index, info_ref[...], 0.0)).astype(jnp.int32)
+    return [at(FLAG_ROWS + k) for k in range(offset_total)], [at(k) for k in range(offset_total)]
+
+
+def pack(pieces, info, offset_total, group, turns):
     slots = slot_total(group, offset_total)
     piece_blocks = pieces[0].shape[0]
 
-    def kernel(offsets_ref, side_ref, *refs):
+    def kernel(info_ref, *refs):
         piece_refs, out_refs, held = refs[: len(pieces)], refs[len(pieces) : -1], refs[-1]
         own_row, pair = lax.axis_index("blk"), lax.axis_index("pair")
         for turn, piece_ref in enumerate(piece_refs):
             first = (pair ^ turn) * piece_blocks
             for block in range(piece_blocks):
                 held[first + block] = piece_ref[block]
-        lane = lax.broadcasted_iota(jnp.int32, (FLAG_ROWS, BINS), 1)
-        flags = jnp.zeros((FLAG_ROWS, BINS), jnp.float32)
-        for k in range(offset_total):
-            flags = jnp.where(lane == k, side_ref[0, k].astype(jnp.float32), flags)
-        flags = flags.astype(jnp.bfloat16)
+        offsets, _ = read_info(info_ref, offset_total)
+        flags = info_ref[...].astype(jnp.bfloat16)
 
         def fill(row, out_ref, parts):
             count = BLOCK_CH // parts
             top = pl.multiple_of(part_top(pair, parts) - part_top(pair, 2), count)
             blocks = [row]
             for slot in range(slots):
-                _, _, partner = slot_pair(row, slot, lambda k: offsets_ref[k], group, offset_total)
+                _, _, partner = slot_pair(row, slot, lambda k: offsets[k], group, offset_total)
                 blocks.append(jnp.clip(partner, 0, group - 1))
             for index, block in enumerate(blocks):
                 for part in range(2):
@@ -190,24 +210,27 @@
         out_shape = [jax.ShapeDtypeStruct((group,) + shape(2), jnp.bfloat16)]
     return pl.pallas_call(
         kernel,
-        in_specs=[SMEM_SPEC, SMEM_SPEC] + [VMEM_SPEC] * len(pieces),
+        in_specs=[VMEM_SPEC] * (1 + len(pieces)),
         out_specs=[VMEM_SPEC] * len(out_shape),
         out_shape=out_shape,
         scratch_shapes=[pltpu.VMEM((group, 2, HALF_CH, BINS), jnp.bfloat16)],
         name="pack",
-    )(offsets, source_side, *[in_vmem(piece) for piece in pieces])
-
-
-def describe_slots(row, duo, offsets_ref, side_ref, far_side, group, offset_total):
+    )(*[in_vmem(value) for value in [info, *pieces]])
+
+
+def describe_slots(row, duo, offsets, sides, far_side, group, offset_total):
     found = []
     for a in range(2):
         side, k, other = 0, 0, 0
         for b in range(slot_total(group, offset_total) // 2):
-            here = slot_pair(row, 2 * b + a, lambda j: offsets_ref[j], group, offset_total)
+            here = slot_pair(row, 2 * b + a, lambda j: offsets[j], group, offset_total)
             side, k, other = [jnp.where(duo == b, x, y) for x, y in zip(here, (side, k, other))]
         valid = jnp.logical_and(other >= 0, other < group)
         far = far_side(jnp.clip(other, 0, group - 1), k)
-        own_source = jnp.where(side == 0, side_ref[0, k] == 0, far)
+        own_side = sides[0]
+        for j in range(1, offset_total):
+            own_side = jnp.where(k == j, sides[j], own_side)
+        own_source = jnp.where(side == 0, own_side == 0, far)
         found.append((side, k, valid, own_source))
     return found
 
@@ -248,12 +271,11 @@
     )
 
 
-def lag_values(totals, a, span, normalizer, turned, put):
+def lag_values(total, a, span, turned, put):
     columns = slice(a * BLOCK_CH, (a + 1) * BLOCK_CH)
 
     def rows(at):
-        found = [total[at * BLOCK_CH : (at + 1) * BLOCK_CH, columns] for total in totals]
-        return sum(found[1:], found[0]) * normalizer
+        return total[at * BLOCK_CH : (at + 1) * BLOCK_CH, columns]
 
     for m in range(span):
         even, odd = rows(m), rows(span + m)
@@ -269,8 +291,7 @@
     ]
 
 
-def correlate_all(mine, theirs, offsets, source_side, group, pairs):
-    offset_total = offsets.shape[0]
+def correlate_all(mine, theirs, info, offset_total, group, pairs):
     slots = slot_total(group, offset_total)
     segs = mine.shape[0]
     steps = segs // SEGS_PER_STEP
@@ -279,7 +300,8 @@
     normalizer = 1.0 / math.sqrt(segs * BINS)
     total_shape = (2 * span * BLOCK_CH, 2 * BLOCK_CH)
 
-    def kernel(offsets_ref, side_ref, *refs):
+    def kernel(info_ref, *refs):
+        offsets, sides = read_info(info_ref, offset_total)
         tables, (mine_ref, theirs_ref, flags_ref, first_ref, second_ref, left, right, total) = refs[:3], refs[3:]
         duo, step = pl.program_id(0), pl.program_id(1)
         row, pair = lax.axis_index("blk"), lax.axis_index("pair")
@@ -288,7 +310,7 @@
         def far_side(other, k):
             return jnp.max(jnp.where(lane == k, flags_ref[other].astype(jnp.float32), 0.0)) > 0.5
 
-        found = describe_slots(row, duo, offsets_ref, side_ref, far_side, group, offset_total)
+        found = describe_slots(row, duo, offsets, sides, far_side, group, offset_total)
 
         @pl.when(jnp.logical_and(duo == 0, step == 0))
         def _():
@@ -319,7 +341,7 @@
                         def put(lag, value):
                             out_ref[0, k, lag] = value
 
-                        lag_values([total], a, span, normalizer, turned, put)
+                        lag_values(total, a, span, turned, put)
 
     out_shape = (1, offset_total, lag_local, BLOCK_CH, BLOCK_CH)
     out_spec = pl.BlockSpec(out_shape, lambda a, b: (0, 0, 0, 0, 0))
@@ -329,16 +351,15 @@
     return pl.pallas_call(
         kernel,
         grid=(slots // 2, steps),
-        in_specs=[SMEM_SPEC, SMEM_SPEC] + [VMEM_SPEC] * 3 + [piece, piece, flags],
+        in_specs=[VMEM_SPEC] * 4 + [piece, piece, flags],
         out_specs=[out_spec] * 2,
         out_shape=[jax.ShapeDtypeStruct(out_shape, jnp.bfloat16)] * 2,
         scratch_shapes=factor_scratch(SEGS_PER_STEP, span) + [pltpu.VMEM(total_shape, jnp.float32)],
         name="correlate",
-    )(offsets, source_side, *lag_tables(pairs), mine, theirs, mine)
-
-
-def correlate_turns(turns, segments, offsets, source_side, group, pairs):
-    offset_total = offsets.shape[0]
+    )(in_vmem(info), *lag_tables(pairs, normalizer), mine, theirs, mine)
+
+
+def correlate_turns(turns, segments, info, offset_total, group, pairs):
     slots = slot_total(group, offset_total)
     lag_local = LAGS // pairs
     span = lag_local // 2
@@ -347,7 +368,8 @@
     out_shape = (1, offset_total, lag_local, BLOCK_CH, BLOCK_CH)
     counts = [len(parts) for parts in segments]
 
-    def kernel(offsets_ref, side_ref, *refs):
+    def kernel(info_ref, *refs):
+        offsets, sides = read_info(info_ref, offset_total)
         tables, refs = refs[:3], refs[3:]
         held = []
         for count in counts:
@@ -364,12 +386,12 @@
                 flags = jnp.where(row ^ turn == other, piece, flags)
             return jnp.max(jnp.where(lane == k, flags, 0.0)) > 0.5
 
-        found = describe_slots(row, 0, offsets_ref, side_ref, far_side, group, offset_total)
+        found = describe_slots(row, 0, offsets, sides, far_side, group, offset_total)
 
         slabs = []
         for side, out_hbm in enumerate((first_hbm, second_hbm)):
             for k in range(offset_total):
-                pair_row = row - offsets_ref[k] if side else row + offsets_ref[k]
+                pair_row = row - offsets[k] if side else row + offsets[k]
                 is_pair = jnp.logical_and(pair_row >= 0, pair_row < group)
                 copy = pltpu.make_async_copy(zeros, out_hbm.at[0, k], zero_sems.at[side, k])
                 slabs.append((jnp.logical_not(is_pair), copy))
@@ -395,7 +417,7 @@
                         pl.when(side == 0)(copy_to(first_hbm, a, k, lag).start)
                         pl.when(side != 0)(copy_to(second_hbm, a, k, lag).start)
 
-                    lag_values([total], a, span, normalizer, turned, put)
+                    lag_values(total, a, span, turned, put)
 
         for a, (side, k, valid, own_source) in enumerate(found):
 
@@ -411,7 +433,7 @@
     operands = [in_vmem(part) for parts in segments for part in parts]
     return pl.pallas_call(
         kernel,
-        in_specs=[SMEM_SPEC, SMEM_SPEC] + [VMEM_SPEC] * (3 + len(operands)),
+        in_specs=[VMEM_SPEC] * (4 + len(operands)),
         out_specs=[any_spec] * 2,
         out_shape=[jax.ShapeDtypeStruct(out_shape, jnp.bfloat16)] * 2,
         scratch_shapes=factor_scratch(len(turns), span)
@@ -423,7 +445,7 @@
             pltpu.SemaphoreType.DMA((2, offset_total)),
         ],
         name="correlate",
-    )(offsets, source_side, *lag_tables(pairs), *operands)
+    )(*[in_vmem(value) for value in [info, *lag_tables(pairs, normalizer)]], *operands)
 
 
 def local(records, offsets, source_side):
@@ -434,22 +456,24 @@
     def swap(value, axis, turn):
         return lax.ppermute(value, axis, [(a, a ^ turn) for a in range(lax.axis_size(axis))])
 
-    mine, other = whiten(records.reshape(records.shape[1], SAMPLES), half_of)
+    offset_total = offsets.shape[0]
+    traces = records.reshape(records.shape[1], SAMPLES)
+    mine, other, info = whiten(traces, offsets, source_side, half_of)
     pieces = [mine]
     for turn in range(1, pairs):
         pieces.append(swap(other if turn % 2 else mine, "pair", turn))
     turns = turns_of(group, pairs)
-    packed = pack(pieces, offsets, source_side, group, turns)
+    packed = pack(pieces, info, offset_total, group, turns)
     if not turns:
         arrived = lax.all_to_all(packed[0], "blk", split_axis=0, concat_axis=0, tiled=True)
         theirs = swap(arrived, "pair", 1)
-        return correlate_all(arrived, theirs, offsets, source_side, group, pairs)
+        return correlate_all(arrived, theirs, info, offset_total, group, pairs)
     segments = []
     for (turn, parts), value in zip(turns, packed):
         arrived = swap(value, "blk", turn) if turn else value
         hops = [swap(arrived, "pair", hop) for hop in range(1, parts)]
         segments.append([arrived] + hops)
-    return correlate_turns(turns, segments, offsets, source_side, group, pairs)
+    return correlate_turns(turns, segments, info, offset_total, group, pairs)
 
 
 def turns_of(group, pairs):

time: 40.4 us -> 38.9 us (0.963)
  Pallas kernels: 7.67 us -> 6.2 us
    pallas_call x2, Pallas kernels: 4.76 us -> 3.51 us  [the longest x1 3.32 us: correlate_turns(): pl.pallas_call(kernel, in_specs=[VMEM_SPEC] * (4 + len(operands)), out_sp...]
where the time goes in v1:
time: 38.9 us; the launch traced here: 38.8 us
  starting transfers between devices  19.6 us (50%)
  waiting for transfers between devices  12.2 us (31%)
  Pallas kernels  6.2 us (16%)
  between operations  0.7 us (2%)
    ppermute x22, starting transfers between devices, swap(): lax.ppermute(value, axis, [(a, a ^ turn) for a in range(lax.axis_size(axi...  19.6 us
    ppermute x22, waiting for transfers between devices, swap(): lax.ppermute(value, axis, [(a, a ^ turn) for a in range(lax.axis_size(axi...  12.2 us
    pallas_call x1, Pallas kernels, correlate_turns(): pl.pallas_call(kernel, in_specs=[VMEM_SPEC] * (4 + len(operands)), out_sp...  3.32 us
    pallas_call x1, Pallas kernels, whiten(): pl.pallas_call(kernel, grid=(blocks // step_blocks,), in_specs=[pl.BlockS...  2.69 us
  transfers between devices with their start and end apart: 22, of which 12 were waited for; matrix products, arithmetic and copies ran while one was open for 0% of the time, Pallas kernels for 0%

profile of v1, /device:TPU:0, one launch (start us, length us, event | category | flops | bytes accessed | tf_op | source)
XLA Modules:
  0.0 38.8 jit_solution(11792943664264452389)
XLA Ops:
  0.7 2.7 %whiten.1 = (bf16[2,2,64,128]{3,2,1,0:T(8,128)(2,1)S(1)}, bf16[2,2,64,128]{3,2,1,0:T(8,128)(2,1)S(1)}, f32[8,128]{1,0:T(8,128)S(1)}) custom-call(s32[2]{0:T(128)} %offsets_hbm.1, s32[1,2]{1,0:T(1,128)} %side_hbm.1, bf16[256,2048]{1,0:T(8,128)(2,1)} %bitcast.1, bf16[2048,512]{1,0:T(8,128)(2,1)} %constant.8.clone.table_hbm), custom_call_target="tpu_custom_call" | custom-call | tf_op jit(solution)/shard_map/whiten/pallas_call | solution.py:107
  3.4 3.1 %collective-permute-start.1 = (bf16[2,2,64,128]{3,2,1,0:T(8,128)(2,1)S(1)}, bf16[2,2,64,128]{3,2,1,0:T(8,128)(2,1)S(1)}, u32[]{:S(2)}, u32[]{:S(2)}) collective-permute-start(bf16[2,2,64,128]{3,2,1,0:T(8,128)(2,1)S(1)} %get-tuple-element.14.refs_0_), channel_id=1, source_target_pairs={{0,2},{1,3},{2,0},{3,1},{4,6},{5,7},{6,4},{7,5},{8,10},{9,11},{10,... | collective-permute-start | bytes 196616 | tf_op jit(solution)/shard_map/ppermute | solution.py:457
  6.6 2.1 %collective-permute-done.1.refs_2_ = bf16[2,2,64,128]{3,2,1,0:T(8,128)(2,1)S(1)} collective-permute-done((bf16[2,2,64,128]{3,2,1,0:T(8,128)(2,1)S(1)}, bf16[2,2,64,128]{3,2,1,0:T(8,128)(2,1)S(1)}, u32[]{:S(2)}, u32[]{:S(2)}) %collective-permute-start.1) | collective-permute-done | bytes 65568 | tf_op jit(solution)/shard_map/ppermute | solution.py:457
  8.7 1.9 %collective-permute-done.2.refs_3_ = bf16[2,2,64,128]{3,2,1,0:T(8,128)(2,1)S(1)} collective-permute-done((bf16[2,2,64,128]{3,2,1,0:T(8,128)(2,1)S(1)}, bf16[2,2,64,128]{3,2,1,0:T(8,128)(2,1)S(1)}, u32[]{:S(2)}, u32[]{:S(2)}) %collective-permute-start.2) | collective-permute-done | bytes 65568 | tf_op jit(solution)/shard_map/ppermute | solution.py:457
  10.8 1.6 %collective-permute-start.12 = (bf16[392,128]{1,0:T(8,128)(2,1)S(1)}, bf16[392,128]{1,0:T(8,128)(2,1)S(1)}, u32[]{:S(2)}, u32[]{:S(2)}) collective-permute-start(bf16[392,128]{1,0:T(8,128)(2,1)S(1)} %get-tuple-element.19), channel_id=1, source_target_pairs={{0,4},{4,0},{8,12},{12,8},{16,20},{20,16},{24,28},{28,24},{1,5},{5... | collective-permute-start | bytes 301064 | tf_op jit(solution)/shard_map/ppermute | solution.py:457
  12.3 3.6 %collective-permute-start.4 = (bf16[200,128]{1,0:T(8,128)(2,1)S(1)}, bf16[200,128]{1,0:T(8,128)(2,1)S(1)}, u32[]{:S(2)}, u32[]{:S(2)}) collective-permute-start(bf16[200,128]{1,0:T(8,128)(2,1)S(1)} %get-tuple-element.17), channel_id=1, source_target_pairs={{0,24},{4,28},{8,16},{12,20},{16,8},{20,12},{24,0},{28,4},{1,25},{... | collective-permute-start | bytes 153608 | tf_op jit(solution)/shard_map/ppermute | solution.py:457
  15.9 0.7 %collective-permute-start.14 = (bf16[392,128]{1,0:T(8,128)(2,1)S(1)}, bf16[392,128]{1,0:T(8,128)(2,1)S(1)}, u32[]{:S(2)}, u32[]{:S(2)}) collective-permute-start(bf16[392,128]{1,0:T(8,128)(2,1)S(1)} %get-tuple-element.20), channel_id=1, source_target_pairs={{0,12},{4,8},{8,4},{12,0},{16,28},{20,24},{24,20},{28,16},{1,13},{... | collective-permute-start | bytes 301064 | tf_op jit(solution)/shard_map/ppermute | solution.py:457
  16.7 2.6 %collective-permute-start.16 = (bf16[392,128]{1,0:T(8,128)(2,1)S(1)}, bf16[392,128]{1,0:T(8,128)(2,1)S(1)}, u32[]{:S(2)}, u32[]{:S(2)}) collective-permute-start(bf16[392,128]{1,0:T(8,128)(2,1)S(1)} %get-tuple-element.21), channel_id=1, source_target_pairs={{0,20},{4,16},{8,28},{12,24},{16,4},{20,0},{24,12},{28,8},{1,21},{... | collective-permute-start | bytes 301064 | tf_op jit(solution)/shard_map/ppermute | solution.py:457
  19.3 3.1 %collective-permute-start.18 = (bf16[392,128]{1,0:T(8,128)(2,1)S(1)}, bf16[392,128]{1,0:T(8,128)(2,1)S(1)}, u32[]{:S(2)}, u32[]{:S(2)}) collective-permute-start(bf16[392,128]{1,0:T(8,128)(2,1)S(1)} %get-tuple-element.22), channel_id=1, source_target_pairs={{0,28},{4,24},{8,20},{12,16},{16,12},{20,8},{24,4},{28,0},{1,29},{... | collective-permute-start | bytes 301064 | tf_op jit(solution)/shard_map/ppermute | solution.py:457
  22.4 0.2 collective-permute-done.8.refs_9_
  22.6 0.7 %collective-permute-done.14.refs_15_ = bf16[392,128]{1,0:T(8,128)(2,1)S(1)} collective-permute-done((bf16[392,128]{1,0:T(8,128)(2,1)S(1)}, bf16[392,128]{1,0:T(8,128)(2,1)S(1)}, u32[]{:S(2)}, u32[]{:S(2)}) %collective-permute-start.14) | collective-permute-done | bytes 100384 | tf_op jit(solution)/shard_map/ppermute | solution.py:457
  23.3 1.3 %collective-permute-start.7 = (bf16[200,128]{1,0:T(8,128)(2,1)S(1)}, bf16[200,128]{1,0:T(8,128)(2,1)S(1)}, u32[]{:S(2)}, u32[]{:S(2)}) collective-permute-start(bf16[200,128]{1,0:T(8,128)(2,1)S(1)} %collective-permute-done.4.refs_5_), channel_id=1, source_target_pairs={{0,3},{1,2},{2,1},{3,0},{4,7},{5,6},{6,5},{7,4},{8,11},{9,10},{10,... | collective-permute-start | bytes 153608 | tf_op jit(solution)/shard_map/ppermute | solution.py:457
  24.6 2.5 %collective-permute-done.16.refs_17_ = bf16[392,128]{1,0:T(8,128)(2,1)S(1)} collective-permute-done((bf16[392,128]{1,0:T(8,128)(2,1)S(1)}, bf16[392,128]{1,0:T(8,128)(2,1)S(1)}, u32[]{:S(2)}, u32[]{:S(2)}) %collective-permute-start.16) | collective-permute-done | bytes 100384 | tf_op jit(solution)/shard_map/ppermute | solution.py:457
  27.1 1.3 %collective-permute-done.18.refs_19_ = bf16[392,128]{1,0:T(8,128)(2,1)S(1)} collective-permute-done((bf16[392,128]{1,0:T(8,128)(2,1)S(1)}, bf16[392,128]{1,0:T(8,128)(2,1)S(1)}, u32[]{:S(2)}, u32[]{:S(2)}) %collective-permute-start.18) | collective-permute-done | bytes 100384 | tf_op jit(solution)/shard_map/ppermute | solution.py:457
  28.6 1.3 %collective-permute-start.11 = (bf16[200,128]{1,0:T(8,128)(2,1)S(1)}, bf16[200,128]{1,0:T(8,128)(2,1)S(1)}, u32[]{:S(2)}, u32[]{:S(2)}) collective-permute-start(bf16[200,128]{1,0:T(8,128)(2,1)S(1)} %collective-permute-done.8.refs_9_), channel_id=1, source_target_pairs={{0,3},{1,2},{2,1},{3,0},{4,7},{5,6},{6,5},{7,4},{8,11},{9,10},{10,... | collective-permute-start | bytes 153608 | tf_op jit(solution)/shard_map/ppermute | solution.py:457
  29.9 0.6 %collective-permute-start.10 = (bf16[200,128]{1,0:T(8,128)(2,1)S(1)}, bf16[200,128]{1,0:T(8,128)(2,1)S(1)}, u32[]{:S(2)}, u32[]{:S(2)}) collective-permute-start(bf16[200,128]{1,0:T(8,128)(2,1)S(1)} %collective-permute-done.8.refs_9_), channel_id=1, source_target_pairs={{0,2},{1,3},{2,0},{3,1},{4,6},{5,7},{6,4},{7,5},{8,10},{9,11},{10,... | collective-permute-start | bytes 153608 | tf_op jit(solution)/shard_map/ppermute | solution.py:457
  30.5 0.7 %collective-permute-done.6.refs_7_ = bf16[200,128]{1,0:T(8,128)(2,1)S(1)} collective-permute-done((bf16[200,128]{1,0:T(8,128)(2,1)S(1)}, bf16[200,128]{1,0:T(8,128)(2,1)S(1)}, u32[]{:S(2)}, u32[]{:S(2)}) %collective-permute-start.6) | collective-permute-done | bytes 51232 | tf_op jit(solution)/shard_map/ppermute | solution.py:457
  31.2 0.5 %collective-permute-start.15 = (bf16[392,128]{1,0:T(8,128)(2,1)S(1)}, bf16[392,128]{1,0:T(8,128)(2,1)S(1)}, u32[]{:S(2)}, u32[]{:S(2)}) collective-permute-start(bf16[392,128]{1,0:T(8,128)(2,1)S(1)} %collective-permute-done.14.refs_15_), channel_id=1, source_target_pairs={{0,1},{1,0},{2,3},{3,2},{4,5},{5,4},{6,7},{7,6},{8,9},{9,8},{10,11... | collective-permute-start | bytes 301064 | tf_op jit(solution)/shard_map/ppermute | solution.py:457
  31.7 0.5 %collective-permute-done.11.refs_12_ = bf16[200,128]{1,0:T(8,128)(2,1)S(1)} collective-permute-done((bf16[200,128]{1,0:T(8,128)(2,1)S(1)}, bf16[200,128]{1,0:T(8,128)(2,1)S(1)}, u32[]{:S(2)}, u32[]{:S(2)}) %collective-permute-start.11) | collective-permute-done | bytes 51232 | tf_op jit(solution)/shard_map/ppermute | solution.py:457
  32.2 0.5 %collective-permute-start.17 = (bf16[392,128]{1,0:T(8,128)(2,1)S(1)}, bf16[392,128]{1,0:T(8,128)(2,1)S(1)}, u32[]{:S(2)}, u32[]{:S(2)}) collective-permute-start(bf16[392,128]{1,0:T(8,128)(2,1)S(1)} %collective-permute-done.16.refs_17_), channel_id=1, source_target_pairs={{0,1},{1,0},{2,3},{3,2},{4,5},{5,4},{6,7},{7,6},{8,9},{9,8},{10,11... | collective-permute-start | bytes 301064 | tf_op jit(solution)/shard_map/ppermute | solution.py:457
  32.6 1.4 %collective-permute-done.10.refs_11_ = bf16[200,128]{1,0:T(8,128)(2,1)S(1)} collective-permute-done((bf16[200,128]{1,0:T(8,128)(2,1)S(1)}, bf16[200,128]{1,0:T(8,128)(2,1)S(1)}, u32[]{:S(2)}, u32[]{:S(2)}) %collective-permute-start.10) | collective-permute-done | bytes 51232 | tf_op jit(solution)/shard_map/ppermute | solution.py:457
  34.0 0.5 %collective-permute-start.21 = (bf16[392,128]{1,0:T(8,128)(2,1)S(1)}, bf16[392,128]{1,0:T(8,128)(2,1)S(1)}, u32[]{:S(2)}, u32[]{:S(2)}) collective-permute-start(bf16[392,128]{1,0:T(8,128)(2,1)S(1)} %collective-permute-done.20.refs_21_), channel_id=1, source_target_pairs={{0,1},{1,0},{2,3},{3,2},{4,5},{5,4},{6,7},{7,6},{8,9},{9,8},{10,11... | collective-permute-start | bytes 301064 | tf_op jit(solution)/shard_map/ppermute | solution.py:457
  34.5 0.8 %collective-permute-done.19.refs_20_ = bf16[392,128]{1,0:T(8,128)(2,1)S(1)} collective-permute-done((bf16[392,128]{1,0:T(8,128)(2,1)S(1)}, bf16[392,128]{1,0:T(8,128)(2,1)S(1)}, u32[]{:S(2)}, u32[]{:S(2)}) %collective-permute-start.19) | collective-permute-done | bytes 100384 | tf_op jit(solution)/shard_map/ppermute | solution.py:457
  35.5 3.3 %correlate.1 = (bf16[1,2,8,128,128]{4,3,2,1,0:T(8,128)(2,1)}, bf16[1,2,8,128,128]{4,3,2,1,0:T(8,128)(2,1)}) custom-call(f32[8,128]{1,0:T(8,128)S(1)} %get-tuple-element.13.info_ref, f32[4,128]{1,0:T(4,128)S(1)} %copy-done.2, f32[4,128]{1,0:T(4,128)S(1)} %copy-done.1, f32[3,4,128]{2,1,0:T(4,128)S(1)} %copy-done, ...), custom_call_target="tpu_custom_call" | custom-call | tf_op jit(solution)/shard_map/correlate/pallas_call | solution.py:434
  (29 shorter events, 0.8 us)
Async XLA Ops:
  0.6 34.8 %copy-start = (f32[3,4,128]{2,1,0:T(4,128)S(1)}, f32[3,4,128]{2,1,0:T(4,128)}, u32[]{:S(2)}) copy-start(f32[3,4,128]{2,1,0:T(4,128)} %constant.11.clone.refs_2_) | copy-start | bytes 18436
  0.6 34.8 %copy-start.1 = (f32[4,128]{1,0:T(4,128)S(1)}, f32[4,128]{1,0:T(4,128)}, u32[]{:S(2)}) copy-start(f32[4,128]{1,0:T(4,128)} %constant.10.clone.refs_1_) | copy-start | bytes 6148
  3.4 5.3 %collective-permute-start.1 = (bf16[2,2,64,128]{3,2,1,0:T(8,128)(2,1)S(1)}, bf16[2,2,64,128]{3,2,1,0:T(8,128)(2,1)S(1)}, u32[]{:S(2)}, u32[]{:S(2)}) collective-permute-start(bf16[2,2,64,128]{3,2,1,0:T(8,128)(2,1)S(1)} %get-tuple-element.14.refs_0_), channel_id=1, source_target_pairs={{0,2},{1,3},{2,0},{3,1},{4,6},{5,7},{6,4},{7,5},{8,10},{9,11},{10,... | collective-permute-start | bytes 196616 | tf_op jit(solution)/shard_map/ppermute | solution.py:457
  6.4 4.1 %collective-permute-start.2 = (bf16[2,2,64,128]{3,2,1,0:T(8,128)(2,1)S(1)}, bf16[2,2,64,128]{3,2,1,0:T(8,128)(2,1)S(1)}, u32[]{:S(2)}, u32[]{:S(2)}) collective-permute-start(bf16[2,2,64,128]{3,2,1,0:T(8,128)(2,1)S(1)} %get-tuple-element.15), channel_id=1, source_target_pairs={{0,3},{1,2},{2,1},{3,0},{4,7},{5,6},{6,5},{7,4},{8,11},{9,10},{10,... | collective-permute-start | bytes 196616 | tf_op jit(solution)/shard_map/ppermute | solution.py:457
  6.4 4.1 %collective-permute-start = (bf16[2,2,64,128]{3,2,1,0:T(8,128)(2,1)S(1)}, bf16[2,2,64,128]{3,2,1,0:T(8,128)(2,1)S(1)}, u32[]{:S(2)}, u32[]{:S(2)}) collective-permute-start(bf16[2,2,64,128]{3,2,1,0:T(8,128)(2,1)S(1)} %get-tuple-element.15), channel_id=1, source_target_pairs={{0,1},{1,0},{2,3},{3,2},{4,5},{5,4},{6,7},{7,6},{8,9},{9,8},{10,11... | collective-permute-start | bytes 196616 | tf_op jit(solution)/shard_map/ppermute | solution.py:457
  10.8 11.9 %collective-permute-start.12 = (bf16[392,128]{1,0:T(8,128)(2,1)S(1)}, bf16[392,128]{1,0:T(8,128)(2,1)S(1)}, u32[]{:S(2)}, u32[]{:S(2)}) collective-permute-start(bf16[392,128]{1,0:T(8,128)(2,1)S(1)} %get-tuple-element.19), channel_id=1, source_target_pairs={{0,4},{4,0},{8,12},{12,8},{16,20},{20,16},{24,28},{28,24},{1,5},{5... | collective-permute-start | bytes 301064 | tf_op jit(solution)/shard_map/ppermute | solution.py:457
  12.3 7.0 %collective-permute-start.4 = (bf16[200,128]{1,0:T(8,128)(2,1)S(1)}, bf16[200,128]{1,0:T(8,128)(2,1)S(1)}, u32[]{:S(2)}, u32[]{:S(2)}) collective-permute-start(bf16[200,128]{1,0:T(8,128)(2,1)S(1)} %get-tuple-element.17), channel_id=1, source_target_pairs={{0,24},{4,28},{8,16},{12,20},{16,8},{20,12},{24,0},{28,4},{1,25},{... | collective-permute-start | bytes 153608 | tf_op jit(solution)/shard_map/ppermute | solution.py:457
  15.9 6.7 %collective-permute-start.8 = (bf16[200,128]{1,0:T(8,128)(2,1)S(1)}, bf16[200,128]{1,0:T(8,128)(2,1)S(1)}, u32[]{:S(2)}, u32[]{:S(2)}) collective-permute-start(bf16[200,128]{1,0:T(8,128)(2,1)S(1)} %get-tuple-element.18), channel_id=1, source_target_pairs={{0,16},{4,20},{8,24},{12,28},{16,0},{20,4},{24,8},{28,12},{1,17},{... | collective-permute-start | bytes 153608 | tf_op jit(solution)/shard_map/ppermute | solution.py:457
  15.9 7.3 %collective-permute-start.14 = (bf16[392,128]{1,0:T(8,128)(2,1)S(1)}, bf16[392,128]{1,0:T(8,128)(2,1)S(1)}, u32[]{:S(2)}, u32[]{:S(2)}) collective-permute-start(bf16[392,128]{1,0:T(8,128)(2,1)S(1)} %get-tuple-element.20), channel_id=1, source_target_pairs={{0,12},{4,8},{8,4},{12,0},{16,28},{20,24},{24,20},{28,16},{1,13},{... | collective-permute-start | bytes 301064 | tf_op jit(solution)/shard_map/ppermute | solution.py:457
  16.7 10.4 %collective-permute-start.16 = (bf16[392,128]{1,0:T(8,128)(2,1)S(1)}, bf16[392,128]{1,0:T(8,128)(2,1)S(1)}, u32[]{:S(2)}, u32[]{:S(2)}) collective-permute-start(bf16[392,128]{1,0:T(8,128)(2,1)S(1)} %get-tuple-element.21), channel_id=1, source_target_pairs={{0,20},{4,16},{8,28},{12,24},{16,4},{20,0},{24,12},{28,8},{1,21},{... | collective-permute-start | bytes 301064 | tf_op jit(solution)/shard_map/ppermute | solution.py:457
  19.3 9.0 %collective-permute-start.18 = (bf16[392,128]{1,0:T(8,128)(2,1)S(1)}, bf16[392,128]{1,0:T(8,128)(2,1)S(1)}, u32[]{:S(2)}, u32[]{:S(2)}) collective-permute-start(bf16[392,128]{1,0:T(8,128)(2,1)S(1)} %get-tuple-element.22), channel_id=1, source_target_pairs={{0,28},{4,24},{8,20},{12,16},{16,12},{20,8},{24,4},{28,0},{1,29},{... | collective-permute-start | bytes 301064 | tf_op jit(solution)/shard_map/ppermute | solution.py:457
  22.6 5.9 %collective-permute-start.20 = (bf16[392,128]{1,0:T(8,128)(2,1)S(1)}, bf16[392,128]{1,0:T(8,128)(2,1)S(1)}, u32[]{:S(2)}, u32[]{:S(2)}) collective-permute-start(bf16[392,128]{1,0:T(8,128)(2,1)S(1)} %get-tuple-element.23), channel_id=1, source_target_pairs={{0,8},{4,12},{8,0},{12,4},{16,24},{20,28},{24,16},{28,20},{1,9},{5... | collective-permute-start | bytes 301064 | tf_op jit(solution)/shard_map/ppermute | solution.py:457
  22.6 7.3 %collective-permute-start.3 = (bf16[392,128]{1,0:T(8,128)(2,1)S(1)}, bf16[392,128]{1,0:T(8,128)(2,1)S(1)}, u32[]{:S(2)}, u32[]{:S(2)}) collective-permute-start(bf16[392,128]{1,0:T(8,128)(2,1)S(1)} %get-tuple-element.16.refs_3_), channel_id=1, source_target_pairs={{0,1},{1,0},{2,3},{3,2},{4,5},{5,4},{6,7},{7,6},{8,9},{9,8},{10,11... | collective-permute-start | bytes 301064 | tf_op jit(solution)/shard_map/ppermute | solution.py:457
  23.3 7.2 %collective-permute-start.7 = (bf16[200,128]{1,0:T(8,128)(2,1)S(1)}, bf16[200,128]{1,0:T(8,128)(2,1)S(1)}, u32[]{:S(2)}, u32[]{:S(2)}) collective-permute-start(bf16[200,128]{1,0:T(8,128)(2,1)S(1)} %collective-permute-done.4.refs_5_), channel_id=1, source_target_pairs={{0,3},{1,2},{2,1},{3,0},{4,7},{5,6},{6,5},{7,4},{8,11},{9,10},{10,... | collective-permute-start | bytes 153608 | tf_op jit(solution)/shard_map/ppermute | solution.py:457
  27.0 4.1 %collective-permute-start.6 = (bf16[200,128]{1,0:T(8,128)(2,1)S(1)}, bf16[200,128]{1,0:T(8,128)(2,1)S(1)}, u32[]{:S(2)}, u32[]{:S(2)}) collective-permute-start(bf16[200,128]{1,0:T(8,128)(2,1)S(1)} %collective-permute-done.4.refs_5_), channel_id=1, source_target_pairs={{0,2},{1,3},{2,0},{3,1},{4,6},{5,7},{6,4},{7,5},{8,10},{9,11},{10,... | collective-permute-start | bytes 153608 | tf_op jit(solution)/shard_map/ppermute | solution.py:457
  28.3 2.8 %collective-permute-start.5 = (bf16[200,128]{1,0:T(8,128)(2,1)S(1)}, bf16[200,128]{1,0:T(8,128)(2,1)S(1)}, u32[]{:S(2)}, u32[]{:S(2)}) collective-permute-start(bf16[200,128]{1,0:T(8,128)(2,1)S(1)} %collective-permute-done.4.refs_5_), channel_id=1, source_target_pairs={{0,1},{1,0},{2,3},{3,2},{4,5},{5,4},{6,7},{7,6},{8,9},{9,8},{10,11... | collective-permute-start | bytes 153608 | tf_op jit(solution)/shard_map/ppermute | solution.py:457
  28.6 3.6 %collective-permute-start.11 = (bf16[200,128]{1,0:T(8,128)(2,1)S(1)}, bf16[200,128]{1,0:T(8,128)(2,1)S(1)}, u32[]{:S(2)}, u32[]{:S(2)}) collective-permute-start(bf16[200,128]{1,0:T(8,128)(2,1)S(1)} %collective-permute-done.8.refs_9_), channel_id=1, source_target_pairs={{0,3},{1,2},{2,1},{3,0},{4,7},{5,6},{6,5},{7,4},{8,11},{9,10},{10,... | collective-permute-start | bytes 153608 | tf_op jit(solution)/shard_map/ppermute | solution.py:457
  29.9 4.1 %collective-permute-start.10 = (bf16[200,128]{1,0:T(8,128)(2,1)S(1)}, bf16[200,128]{1,0:T(8,128)(2,1)S(1)}, u32[]{:S(2)}, u32[]{:S(2)}) collective-permute-start(bf16[200,128]{1,0:T(8,128)(2,1)S(1)} %collective-permute-done.8.refs_9_), channel_id=1, source_target_pairs={{0,2},{1,3},{2,0},{3,1},{4,6},{5,7},{6,4},{7,5},{8,10},{9,11},{10,... | collective-permute-start | bytes 153608 | tf_op jit(solution)/shard_map/ppermute | solution.py:457
  30.5 3.5 %collective-permute-start.9 = (bf16[200,128]{1,0:T(8,128)(2,1)S(1)}, bf16[200,128]{1,0:T(8,128)(2,1)S(1)}, u32[]{:S(2)}, u32[]{:S(2)}) collective-permute-start(bf16[200,128]{1,0:T(8,128)(2,1)S(1)} %collective-permute-done.8.refs_9_), channel_id=1, source_target_pairs={{0,1},{1,0},{2,3},{3,2},{4,5},{5,4},{6,7},{7,6},{8,9},{9,8},{10,11... | collective-permute-start | bytes 153608 | tf_op jit(solution)/shard_map/ppermute | solution.py:457
  31.2 3.3 %collective-permute-start.13 = (bf16[392,128]{1,0:T(8,128)(2,1)S(1)}, bf16[392,128]{1,0:T(8,128)(2,1)S(1)}, u32[]{:S(2)}, u32[]{:S(2)}) collective-permute-start(bf16[392,128]{1,0:T(8,128)(2,1)S(1)} %collective-permute-done.12.refs_13_), channel_id=1, source_target_pairs={{0,1},{1,0},{2,3},{3,2},{4,5},{5,4},{6,7},{7,6},{8,9},{9,8},{10,11... | collective-permute-start | bytes 301064 | tf_op jit(solution)/shard_map/ppermute | solution.py:457
  31.2 3.3 %collective-permute-start.15 = (bf16[392,128]{1,0:T(8,128)(2,1)S(1)}, bf16[392,128]{1,0:T(8,128)(2,1)S(1)}, u32[]{:S(2)}, u32[]{:S(2)}) collective-permute-start(bf16[392,128]{1,0:T(8,128)(2,1)S(1)} %collective-permute-done.14.refs_15_), channel_id=1, source_target_pairs={{0,1},{1,0},{2,3},{3,2},{4,5},{5,4},{6,7},{7,6},{8,9},{9,8},{10,11... | collective-permute-start | bytes 301064 | tf_op jit(solution)/shard_map/ppermute | solution.py:457
  32.2 2.4 %collective-permute-start.17 = (bf16[392,128]{1,0:T(8,128)(2,1)S(1)}, bf16[392,128]{1,0:T(8,128)(2,1)S(1)}, u32[]{:S(2)}, u32[]{:S(2)}) collective-permute-start(bf16[392,128]{1,0:T(8,128)(2,1)S(1)} %collective-permute-done.16.refs_17_), channel_id=1, source_target_pairs={{0,1},{1,0},{2,3},{3,2},{4,5},{5,4},{6,7},{7,6},{8,9},{9,8},{10,11... | collective-permute-start | bytes 301064 | tf_op jit(solution)/shard_map/ppermute | solution.py:457
  34.0 1.3 %collective-permute-start.19 = (bf16[392,128]{1,0:T(8,128)(2,1)S(1)}, bf16[392,128]{1,0:T(8,128)(2,1)S(1)}, u32[]{:S(2)}, u32[]{:S(2)}) collective-permute-start(bf16[392,128]{1,0:T(8,128)(2,1)S(1)} %collective-permute-done.18.refs_19_), channel_id=1, source_target_pairs={{0,1},{1,0},{2,3},{3,2},{4,5},{5,4},{6,7},{7,6},{8,9},{9,8},{10,11... | collective-permute-start | bytes 301064 | tf_op jit(solution)/shard_map/ppermute | solution.py:457
  34.0 1.5 %collective-permute-start.21 = (bf16[392,128]{1,0:T(8,128)(2,1)S(1)}, bf16[392,128]{1,0:T(8,128)(2,1)S(1)}, u32[]{:S(2)}, u32[]{:S(2)}) collective-permute-start(bf16[392,128]{1,0:T(8,128)(2,1)S(1)} %collective-permute-done.20.refs_21_), channel_id=1, source_target_pairs={{0,1},{1,0},{2,3},{3,2},{4,5},{5,4},{6,7},{7,6},{8,9},{9,8},{10,11... | collective-permute-start | bytes 301064 | tf_op jit(solution)/shard_map/ppermute | solution.py:457
  (1 other events, 34.8 us)

commit v2 on v1

--- a/solution.py
+++ b/solution.py
@@ -17,7 +17,8 @@
 HALF_CH = BLOCK_CH // 2
 BLOCKS_PER_STEP = 2
 DEPTH_CHUNKS = 2
-TURNS = ((0, 2), (6, 4), (4, 4), (1, 2), (3, 2), (5, 2), (7, 2), (2, 2))
+TURNS = ((0, 2), (6, 4), (4, 4), (1, 2), (3, 2), (5, 4), (7, 2), (2, 2))
+JOINED = (0, 6, 4)
 SEGS_PER_STEP = 8
 FLAG_ROWS = 8
 VMEM_SPEC = pl.BlockSpec(memory_space=pltpu.VMEM)
@@ -359,6 +360,31 @@
     )(in_vmem(info), *lag_tables(pairs, normalizer), mine, theirs, mine)
 
 
+def join(groups):
+    arrays = [array for group in groups for array in group]
+    counts = [len(group) for group in groups]
+
+    def kernel(*refs):
+        sources, targets = refs[: len(arrays)], refs[len(arrays) :]
+        for count, target in zip(counts, targets):
+            at = 0
+            for source in sources[:count]:
+                target[at : at + source.shape[0]] = source[...]
+                at += source.shape[0]
+            sources = sources[count:]
+
+    out_shape = [
+        pltpu.VMEM((sum(array.shape[0] for array in group), BINS), jnp.bfloat16) for group in groups
+    ]
+    return pl.pallas_call(
+        kernel,
+        in_specs=[VMEM_SPEC] * len(arrays),
+        out_specs=[VMEM_SPEC] * len(groups),
+        out_shape=out_shape,
+        name="join",
+    )(*[in_vmem(array) for array in arrays])
+
+
 def correlate_turns(turns, segments, info, offset_total, group, pairs):
     slots = slot_total(group, offset_total)
     lag_local = LAGS // pairs
@@ -366,15 +392,20 @@
     normalizer = 1.0 / math.sqrt(len(turns) * BINS)
     total_shape = (2 * span * BLOCK_CH, 2 * BLOCK_CH)
     out_shape = (1, offset_total, lag_local, BLOCK_CH, BLOCK_CH)
-    counts = [len(parts) for parts in segments]
+    arrays = []
+    for parts in segments:
+        arrays += [array for array, _ in parts if all(array is not other for other in arrays)]
+    index_of = lambda array: [array is other for other in arrays].index(True)
+    places = [[(index_of(array), at) for array, at in parts] for parts in segments]
 
     def kernel(info_ref, *refs):
         offsets, sides = read_info(info_ref, offset_total)
         tables, refs = refs[:3], refs[3:]
         held = []
-        for count in counts:
-            held.append(refs[:count])
-            refs = refs[count:]
+        for parts in places:
+            rows = flag_at(slots, len(parts)) + FLAG_ROWS
+            held.append([refs[index].at[at : at + rows] for index, at in parts])
+        refs = refs[len(arrays) :]
         first_hbm, second_hbm, left, right, total, result, zeros, sems, zero_sems = refs
         row, pair = lax.axis_index("blk"), lax.axis_index("pair")
         lane = lax.broadcasted_iota(jnp.int32, (FLAG_ROWS, BINS), 1)
@@ -430,7 +461,7 @@
             pl.when(blank)(copy.wait)
 
     any_spec = pl.BlockSpec(memory_space=pl.ANY)
-    operands = [in_vmem(part) for parts in segments for part in parts]
+    operands = [in_vmem(array) for array in arrays]
     return pl.pallas_call(
         kernel,
         in_specs=[VMEM_SPEC] * (4 + len(operands)),
@@ -468,11 +499,27 @@
         arrived = lax.all_to_all(packed[0], "blk", split_axis=0, concat_axis=0, tiled=True)
         theirs = swap(arrived, "pair", 1)
         return correlate_all(arrived, theirs, info, offset_total, group, pairs)
+    parts_of = dict(turns)
+    arrived = {}
+    for (turn, _), value in zip(turns, packed):
+        arrived[turn] = swap(value, "blk", turn) if turn else value
+    quarters = [turn for turn in JOINED if parts_of[turn] == 4]
+    below, both = join([[arrived[turn] for turn in quarters], [arrived[turn] for turn in JOINED]])
+    below_2 = swap(below, "pair", 2)
+    both_1 = swap(both, "pair", 1)
+    below_3 = swap(below_2, "pair", 1)
     segments = []
-    for (turn, parts), value in zip(turns, packed):
-        arrived = swap(value, "blk", turn) if turn else value
-        hops = [swap(arrived, "pair", hop) for hop in range(1, parts)]
-        segments.append([arrived] + hops)
+    for turn, parts in turns:
+        if turn in JOINED:
+            ahead = JOINED[: JOINED.index(turn)]
+            found = [(arrived[turn], 0), (both_1, sum(arrived[other].shape[0] for other in ahead))]
+            if parts == 4:
+                at = sum(arrived[other].shape[0] for other in ahead if other in quarters)
+                found += [(below_2, at), (below_3, at)]
+        else:
+            hops = [swap(arrived[turn], "pair", hop) for hop in range(1, parts)]
+            found = [(array, 0) for array in [arrived[turn]] + hops]
+        segments.append(found)
     return correlate_turns(turns, segments, info, offset_total, group, pairs)
 
 

time: 38.9 us -> 39.5 us (1.015)
  waiting for transfers between devices: 12.2 us -> 13.3 us
    ppermute x22 -> x20, waiting for transfers between devices: 12.2 us -> 13.3 us  [swap(): lax.ppermute(value, axis, [(a, a ^ turn) for a in range(lax.axis_size(axi...]
    ppermute x22 -> x20, starting transfers between devices: 19.6 us -> 19.3 us  [swap(): lax.ppermute(value, axis, [(a, a ^ turn) for a in range(lax.axis_size(axi...]
  transfers between devices with their start and end apart: 22 -> 20, of which waited for: 12 -> 9; matrix products, arithmetic and copies ran while one was open for 0% -> 0% of each run, Pallas kernels for 0% -> 0%
where the time goes in v2:
time: 39.5 us; the launch traced here: 39.4 us
  starting transfers between devices  19.3 us (49%)
  waiting for transfers between devices  13.3 us (34%)
  Pallas kernels  6.06 us (15%)
  between operations  0.72 us (2%)
    ppermute x20, starting transfers between devices, swap(): lax.ppermute(value, axis, [(a, a ^ turn) for a in range(lax.axis_size(axi...  19.3 us
    ppermute x20, waiting for transfers between devices, swap(): lax.ppermute(value, axis, [(a, a ^ turn) for a in range(lax.axis_size(axi...  13.3 us
    pallas_call x1, Pallas kernels, correlate_turns(): pl.pallas_call(kernel, in_specs=[VMEM_SPEC] * (4 + len(operands)), out_sp...  3.16 us
    pallas_call x1, Pallas kernels, whiten(): pl.pallas_call(kernel, grid=(blocks // step_blocks,), in_specs=[pl.BlockS...  2.69 us
  transfers between devices with their start and end apart: 20, of which 9 were waited for; matrix products, arithmetic and copies ran while one was open for 0% of the time, Pallas kernels for 0%

profile of v2, /device:TPU:0, one launch (start us, length us, event | category | flops | bytes accessed | tf_op | source)
XLA Modules:
  0.0 39.4 jit_solution(9585905335997983569)
XLA Ops:
  0.7 2.7 %whiten.1 = (bf16[2,2,64,128]{3,2,1,0:T(8,128)(2,1)S(1)}, bf16[2,2,64,128]{3,2,1,0:T(8,128)(2,1)S(1)}, f32[8,128]{1,0:T(8,128)S(1)}) custom-call(s32[2]{0:T(128)} %offsets_hbm.1, s32[1,2]{1,0:T(1,128)} %side_hbm.1, bf16[256,2048]{1,0:T(8,128)(2,1)} %bitcast.1, bf16[2048,512]{1,0:T(8,128)(2,1)} %constant.8.clone.table_hbm), custom_call_target="tpu_custom_call" | custom-call | tf_op jit(solution)/shard_map/whiten/pallas_call | solution.py:108
  3.4 3.1 %collective-permute-start.1 = (bf16[2,2,64,128]{3,2,1,0:T(8,128)(2,1)S(1)}, bf16[2,2,64,128]{3,2,1,0:T(8,128)(2,1)S(1)}, u32[]{:S(2)}, u32[]{:S(2)}) collective-permute-start(bf16[2,2,64,128]{3,2,1,0:T(8,128)(2,1)S(1)} %get-tuple-element.16.refs_0_), channel_id=1, source_target_pairs={{0,2},{1,3},{2,0},{3,1},{4,6},{5,7},{6,4},{7,5},{8,10},{9,11},{10,... | collective-permute-start | bytes 196616 | tf_op jit(solution)/shard_map/ppermute | solution.py:488
  6.4 0.2 collective-permute-start
  6.6 2.1 %collective-permute-done.1.refs_2_ = bf16[2,2,64,128]{3,2,1,0:T(8,128)(2,1)S(1)} collective-permute-done((bf16[2,2,64,128]{3,2,1,0:T(8,128)(2,1)S(1)}, bf16[2,2,64,128]{3,2,1,0:T(8,128)(2,1)S(1)}, u32[]{:S(2)}, u32[]{:S(2)}) %collective-permute-start.1) | collective-permute-done | bytes 65568 | tf_op jit(solution)/shard_map/ppermute | solution.py:488
  8.7 1.9 %collective-permute-done.2.refs_3_ = bf16[2,2,64,128]{3,2,1,0:T(8,128)(2,1)S(1)} collective-permute-done((bf16[2,2,64,128]{3,2,1,0:T(8,128)(2,1)S(1)}, bf16[2,2,64,128]{3,2,1,0:T(8,128)(2,1)S(1)}, u32[]{:S(2)}, u32[]{:S(2)}) %collective-permute-start.2) | collective-permute-done | bytes 65568 | tf_op jit(solution)/shard_map/ppermute | solution.py:488
  10.6 0.2 pack.1
  10.8 3.7 %collective-permute-start.3 = (bf16[200,128]{1,0:T(8,128)(2,1)S(1)}, bf16[200,128]{1,0:T(8,128)(2,1)S(1)}, u32[]{:S(2)}, u32[]{:S(2)}) collective-permute-start(bf16[200,128]{1,0:T(8,128)(2,1)S(1)} %get-tuple-element.19), channel_id=1, source_target_pairs={{0,24},{4,28},{8,16},{12,20},{16,8},{20,12},{24,0},{28,4},{1,25},{... | collective-permute-start | bytes 153608 | tf_op jit(solution)/shard_map/ppermute | solution.py:488
  14.4 1.5 %collective-permute-start.8 = (bf16[392,128]{1,0:T(8,128)(2,1)S(1)}, bf16[392,128]{1,0:T(8,128)(2,1)S(1)}, u32[]{:S(2)}, u32[]{:S(2)}) collective-permute-start(bf16[392,128]{1,0:T(8,128)(2,1)S(1)} %get-tuple-element.23), channel_id=1, source_target_pairs={{0,4},{4,0},{8,12},{12,8},{16,20},{20,16},{24,28},{28,24},{1,5},{5... | collective-permute-start | bytes 301064 | tf_op jit(solution)/shard_map/ppermute | solution.py:488
  15.9 0.7 %collective-permute-start.10 = (bf16[392,128]{1,0:T(8,128)(2,1)S(1)}, bf16[392,128]{1,0:T(8,128)(2,1)S(1)}, u32[]{:S(2)}, u32[]{:S(2)}) collective-permute-start(bf16[392,128]{1,0:T(8,128)(2,1)S(1)} %get-tuple-element.24), channel_id=1, source_target_pairs={{0,12},{4,8},{8,4},{12,0},{16,28},{20,24},{24,20},{28,16},{1,13},{... | collective-permute-start | bytes 301064 | tf_op jit(solution)/shard_map/ppermute | solution.py:488
  16.7 4.5 %collective-permute-start.16 = (bf16[392,128]{1,0:T(8,128)(2,1)S(1)}, bf16[392,128]{1,0:T(8,128)(2,1)S(1)}, u32[]{:S(2)}, u32[]{:S(2)}) collective-permute-start(bf16[392,128]{1,0:T(8,128)(2,1)S(1)} %get-tuple-element.26), channel_id=1, source_target_pairs={{0,28},{4,24},{8,20},{12,16},{16,12},{20,8},{24,4},{28,0},{1,29},{... | collective-permute-start | bytes 301064 | tf_op jit(solution)/shard_map/ppermute | solution.py:488
  21.2 0.9 %collective-permute-start.18 = (bf16[392,128]{1,0:T(8,128)(2,1)S(1)}, bf16[392,128]{1,0:T(8,128)(2,1)S(1)}, u32[]{:S(2)}, u32[]{:S(2)}) collective-permute-start(bf16[392,128]{1,0:T(8,128)(2,1)S(1)} %get-tuple-element.27), channel_id=1, source_target_pairs={{0,8},{4,12},{8,0},{12,4},{16,24},{20,28},{24,16},{28,20},{1,9},{5... | collective-permute-start | bytes 301064 | tf_op jit(solution)/shard_map/ppermute | solution.py:488
  22.1 5.4 %collective-permute-done.12.refs_13_ = bf16[200,128]{1,0:T(8,128)(2,1)S(1)} collective-permute-done((bf16[200,128]{1,0:T(8,128)(2,1)S(1)}, bf16[200,128]{1,0:T(8,128)(2,1)S(1)}, u32[]{:S(2)}, u32[]{:S(2)}) %collective-permute-start.12) | collective-permute-done | bytes 51232 | tf_op jit(solution)/shard_map/ppermute | solution.py:488
  27.5 1.2 %collective-permute-start.6 = (bf16[400,128]{1,0:T(8,128)(2,1)S(1)}, bf16[400,128]{1,0:T(8,128)(2,1)S(1)}, u32[]{:S(2)}, u32[]{:S(2)}) collective-permute-start(bf16[400,128]{1,0:T(8,128)(2,1)S(1)} %get-tuple-element.22), channel_id=1, source_target_pairs={{0,2},{1,3},{2,0},{3,1},{4,6},{5,7},{6,4},{7,5},{8,10},{9,11},{10,... | collective-permute-start | bytes 307208 | tf_op jit(solution)/shard_map/ppermute | solution.py:488
  28.7 0.9 %collective-permute-start.5 = (bf16[792,128]{1,0:T(8,128)(2,1)S(1)}, bf16[792,128]{1,0:T(8,128)(2,1)S(1)}, u32[]{:S(2)}, u32[]{:S(2)}) collective-permute-start(bf16[792,128]{1,0:T(8,128)(2,1)S(1)} %get-tuple-element.21), channel_id=1, source_target_pairs={{0,1},{1,0},{2,3},{3,2},{4,5},{5,4},{6,7},{7,6},{8,9},{9,8},{10,11... | collective-permute-start | bytes 608264 | tf_op jit(solution)/shard_map/ppermute | solution.py:488
  29.7 1.2 %collective-permute-start.14 = (bf16[200,128]{1,0:T(8,128)(2,1)S(1)}, bf16[200,128]{1,0:T(8,128)(2,1)S(1)}, u32[]{:S(2)}, u32[]{:S(2)}) collective-permute-start(bf16[200,128]{1,0:T(8,128)(2,1)S(1)} %collective-permute-done.12.refs_13_), channel_id=1, source_target_pairs={{0,2},{1,3},{2,0},{3,1},{4,6},{5,7},{6,4},{7,5},{8,10},{9,11},{10,... | collective-permute-start | bytes 153608 | tf_op jit(solution)/shard_map/ppermute | solution.py:488
  30.9 1.9 %collective-permute-done.15.refs_16_ = bf16[200,128]{1,0:T(8,128)(2,1)S(1)} collective-permute-done((bf16[200,128]{1,0:T(8,128)(2,1)S(1)}, bf16[200,128]{1,0:T(8,128)(2,1)S(1)}, u32[]{:S(2)}, u32[]{:S(2)}) %collective-permute-start.15) | collective-permute-done | bytes 51232 | tf_op jit(solution)/shard_map/ppermute | solution.py:488
  32.8 0.8 %collective-permute-start.13 = (bf16[200,128]{1,0:T(8,128)(2,1)S(1)}, bf16[200,128]{1,0:T(8,128)(2,1)S(1)}, u32[]{:S(2)}, u32[]{:S(2)}) collective-permute-start(bf16[200,128]{1,0:T(8,128)(2,1)S(1)} %collective-permute-done.12.refs_13_), channel_id=1, source_target_pairs={{0,1},{1,0},{2,3},{3,2},{4,5},{5,4},{6,7},{7,6},{8,9},{9,8},{10,11... | collective-permute-start | bytes 153608 | tf_op jit(solution)/shard_map/ppermute | solution.py:488
  33.6 0.8 %collective-permute-done.14.refs_15_ = bf16[200,128]{1,0:T(8,128)(2,1)S(1)} collective-permute-done((bf16[200,128]{1,0:T(8,128)(2,1)S(1)}, bf16[200,128]{1,0:T(8,128)(2,1)S(1)}, u32[]{:S(2)}, u32[]{:S(2)}) %collective-permute-start.14) | collective-permute-done | bytes 51232 | tf_op jit(solution)/shard_map/ppermute | solution.py:488
  34.4 0.1 collective-permute-done.13.refs_14_
  34.4 0.4 %collective-permute-start.17 = (bf16[392,128]{1,0:T(8,128)(2,1)S(1)}, bf16[392,128]{1,0:T(8,128)(2,1)S(1)}, u32[]{:S(2)}, u32[]{:S(2)}) collective-permute-start(bf16[392,128]{1,0:T(8,128)(2,1)S(1)} %collective-permute-done.16.refs_17_), channel_id=1, source_target_pairs={{0,1},{1,0},{2,3},{3,2},{4,5},{5,4},{6,7},{7,6},{8,9},{9,8},{10,11... | collective-permute-start | bytes 301064 | tf_op jit(solution)/shard_map/ppermute | solution.py:488
  34.9 0.7 %collective-permute-done.11.refs_12_ = bf16[392,128]{1,0:T(8,128)(2,1)S(1)} collective-permute-done((bf16[392,128]{1,0:T(8,128)(2,1)S(1)}, bf16[392,128]{1,0:T(8,128)(2,1)S(1)}, u32[]{:S(2)}, u32[]{:S(2)}) %collective-permute-start.11) | collective-permute-done | bytes 100384 | tf_op jit(solution)/shard_map/ppermute | solution.py:488
  35.7 0.2 collective-permute-done.17.refs_18_
  35.8 0.4 collective-permute-done.19.refs_20_
  36.2 3.2 %correlate.1 = (bf16[1,2,8,128,128]{4,3,2,1,0:T(8,128)(2,1)}, bf16[1,2,8,128,128]{4,3,2,1,0:T(8,128)(2,1)}) custom-call(f32[8,128]{1,0:T(8,128)S(1)} %get-tuple-element.15.info_ref, f32[4,128]{1,0:T(4,128)S(1)} %copy-done.2, f32[4,128]{1,0:T(4,128)S(1)} %copy-done.1, f32[3,4,128]{2,1,0:T(4,128)S(1)} %copy-done, ...), custom_call_target="tpu_custom_call" | custom-call | tf_op jit(solution)/shard_map/correlate/pallas_call | solution.py:465
  (26 shorter events, 0.2 us)
Async XLA Ops:
  0.6 35.6 %copy-start = (f32[3,4,128]{2,1,0:T(4,128)S(1)}, f32[3,4,128]{2,1,0:T(4,128)}, u32[]{:S(2)}) copy-start(f32[3,4,128]{2,1,0:T(4,128)} %constant.11.clone.refs_2_) | copy-start | bytes 18436
  0.6 35.5 %copy-start.1 = (f32[4,128]{1,0:T(4,128)S(1)}, f32[4,128]{1,0:T(4,128)}, u32[]{:S(2)}) copy-start(f32[4,128]{1,0:T(4,128)} %constant.10.clone.refs_1_) | copy-start | bytes 6148
  0.7 35.5 %copy-start.2 = (f32[4,128]{1,0:T(4,128)S(1)}, f32[4,128]{1,0:T(4,128)}, u32[]{:S(2)}) copy-start(f32[4,128]{1,0:T(4,128)} %constant.9.clone.refs_0_) | copy-start | bytes 6148
  3.4 5.3 %collective-permute-start.1 = (bf16[2,2,64,128]{3,2,1,0:T(8,128)(2,1)S(1)}, bf16[2,2,64,128]{3,2,1,0:T(8,128)(2,1)S(1)}, u32[]{:S(2)}, u32[]{:S(2)}) collective-permute-start(bf16[2,2,64,128]{3,2,1,0:T(8,128)(2,1)S(1)} %get-tuple-element.16.refs_0_), channel_id=1, source_target_pairs={{0,2},{1,3},{2,0},{3,1},{4,6},{5,7},{6,4},{7,5},{8,10},{9,11},{10,... | collective-permute-start | bytes 196616 | tf_op jit(solution)/shard_map/ppermute | solution.py:488
  6.4 4.1 %collective-permute-start.2 = (bf16[2,2,64,128]{3,2,1,0:T(8,128)(2,1)S(1)}, bf16[2,2,64,128]{3,2,1,0:T(8,128)(2,1)S(1)}, u32[]{:S(2)}, u32[]{:S(2)}) collective-permute-start(bf16[2,2,64,128]{3,2,1,0:T(8,128)(2,1)S(1)} %get-tuple-element.17), channel_id=1, source_target_pairs={{0,3},{1,2},{2,1},{3,0},{4,7},{5,6},{6,5},{7,4},{8,11},{9,10},{10,... | collective-permute-start | bytes 196616 | tf_op jit(solution)/shard_map/ppermute | solution.py:488
  6.4 4.1 %collective-permute-start = (bf16[2,2,64,128]{3,2,1,0:T(8,128)(2,1)S(1)}, bf16[2,2,64,128]{3,2,1,0:T(8,128)(2,1)S(1)}, u32[]{:S(2)}, u32[]{:S(2)}) collective-permute-start(bf16[2,2,64,128]{3,2,1,0:T(8,128)(2,1)S(1)} %get-tuple-element.17), channel_id=1, source_target_pairs={{0,1},{1,0},{2,3},{3,2},{4,5},{5,4},{6,7},{7,6},{8,9},{9,8},{10,11... | collective-permute-start | bytes 196616 | tf_op jit(solution)/shard_map/ppermute | solution.py:488
  10.8 10.5 %collective-permute-start.3 = (bf16[200,128]{1,0:T(8,128)(2,1)S(1)}, bf16[200,128]{1,0:T(8,128)(2,1)S(1)}, u32[]{:S(2)}, u32[]{:S(2)}) collective-permute-start(bf16[200,128]{1,0:T(8,128)(2,1)S(1)} %get-tuple-element.19), channel_id=1, source_target_pairs={{0,24},{4,28},{8,16},{12,20},{16,8},{20,12},{24,0},{28,4},{1,25},{... | collective-permute-start | bytes 153608 | tf_op jit(solution)/shard_map/ppermute | solution.py:488
  14.4 6.8 %collective-permute-start.4 = (bf16[200,128]{1,0:T(8,128)(2,1)S(1)}, bf16[200,128]{1,0:T(8,128)(2,1)S(1)}, u32[]{:S(2)}, u32[]{:S(2)}) collective-permute-start(bf16[200,128]{1,0:T(8,128)(2,1)S(1)} %get-tuple-element.20), channel_id=1, source_target_pairs={{0,16},{4,20},{8,24},{12,28},{16,0},{20,4},{24,8},{28,12},{1,17},{... | collective-permute-start | bytes 153608 | tf_op jit(solution)/shard_map/ppermute | solution.py:488
  14.4 14.2 %collective-permute-start.8 = (bf16[392,128]{1,0:T(8,128)(2,1)S(1)}, bf16[392,128]{1,0:T(8,128)(2,1)S(1)}, u32[]{:S(2)}, u32[]{:S(2)}) collective-permute-start(bf16[392,128]{1,0:T(8,128)(2,1)S(1)} %get-tuple-element.23), channel_id=1, source_target_pairs={{0,4},{4,0},{8,12},{12,8},{16,20},{20,16},{24,28},{28,24},{1,5},{5... | collective-permute-start | bytes 301064 | tf_op jit(solution)/shard_map/ppermute | solution.py:488
  15.9 12.8 %collective-permute-start.10 = (bf16[392,128]{1,0:T(8,128)(2,1)S(1)}, bf16[392,128]{1,0:T(8,128)(2,1)S(1)}, u32[]{:S(2)}, u32[]{:S(2)}) collective-permute-start(bf16[392,128]{1,0:T(8,128)(2,1)S(1)} %get-tuple-element.24), channel_id=1, source_target_pairs={{0,12},{4,8},{8,4},{12,0},{16,28},{20,24},{24,20},{28,16},{1,13},{... | collective-permute-start | bytes 301064 | tf_op jit(solution)/shard_map/ppermute | solution.py:488
  16.7 13.0 %collective-permute-start.16 = (bf16[392,128]{1,0:T(8,128)(2,1)S(1)}, bf16[392,128]{1,0:T(8,128)(2,1)S(1)}, u32[]{:S(2)}, u32[]{:S(2)}) collective-permute-start(bf16[392,128]{1,0:T(8,128)(2,1)S(1)} %get-tuple-element.26), channel_id=1, source_target_pairs={{0,28},{4,24},{8,20},{12,16},{16,12},{20,8},{24,4},{28,0},{1,29},{... | collective-permute-start | bytes 301064 | tf_op jit(solution)/shard_map/ppermute | solution.py:488
  21.2 6.3 %collective-permute-start.12 = (bf16[200,128]{1,0:T(8,128)(2,1)S(1)}, bf16[200,128]{1,0:T(8,128)(2,1)S(1)}, u32[]{:S(2)}, u32[]{:S(2)}) collective-permute-start(bf16[200,128]{1,0:T(8,128)(2,1)S(1)} %get-tuple-element.25), channel_id=1, source_target_pairs={{0,20},{4,16},{8,28},{12,24},{16,4},{20,0},{24,12},{28,8},{1,21},{... | collective-permute-start | bytes 153608 | tf_op jit(solution)/shard_map/ppermute | solution.py:488
  21.2 8.5 %collective-permute-start.18 = (bf16[392,128]{1,0:T(8,128)(2,1)S(1)}, bf16[392,128]{1,0:T(8,128)(2,1)S(1)}, u32[]{:S(2)}, u32[]{:S(2)}) collective-permute-start(bf16[392,128]{1,0:T(8,128)(2,1)S(1)} %get-tuple-element.27), channel_id=1, source_target_pairs={{0,8},{4,12},{8,0},{12,4},{16,24},{20,28},{24,16},{28,20},{1,9},{5... | collective-permute-start | bytes 301064 | tf_op jit(solution)/shard_map/ppermute | solution.py:488
  27.5 6.1 %collective-permute-start.6 = (bf16[400,128]{1,0:T(8,128)(2,1)S(1)}, bf16[400,128]{1,0:T(8,128)(2,1)S(1)}, u32[]{:S(2)}, u32[]{:S(2)}) collective-permute-start(bf16[400,128]{1,0:T(8,128)(2,1)S(1)} %get-tuple-element.22), channel_id=1, source_target_pairs={{0,2},{1,3},{2,0},{3,1},{4,6},{5,7},{6,4},{7,5},{8,10},{9,11},{10,... | collective-permute-start | bytes 307208 | tf_op jit(solution)/shard_map/ppermute | solution.py:488
  28.7 4.1 %collective-permute-start.15 = (bf16[200,128]{1,0:T(8,128)(2,1)S(1)}, bf16[200,128]{1,0:T(8,128)(2,1)S(1)}, u32[]{:S(2)}, u32[]{:S(2)}) collective-permute-start(bf16[200,128]{1,0:T(8,128)(2,1)S(1)} %collective-permute-done.12.refs_13_), channel_id=1, source_target_pairs={{0,3},{1,2},{2,1},{3,0},{4,7},{5,6},{6,5},{7,4},{8,11},{9,10},{10,... | collective-permute-start | bytes 153608 | tf_op jit(solution)/shard_map/ppermute | solution.py:488
  28.7 7.5 %collective-permute-start.5 = (bf16[792,128]{1,0:T(8,128)(2,1)S(1)}, bf16[792,128]{1,0:T(8,128)(2,1)S(1)}, u32[]{:S(2)}, u32[]{:S(2)}) collective-permute-start(bf16[792,128]{1,0:T(8,128)(2,1)S(1)} %get-tuple-element.21), channel_id=1, source_target_pairs={{0,1},{1,0},{2,3},{3,2},{4,5},{5,4},{6,7},{7,6},{8,9},{9,8},{10,11... | collective-permute-start | bytes 608264 | tf_op jit(solution)/shard_map/ppermute | solution.py:488
  29.7 5.2 %collective-permute-start.9 = (bf16[392,128]{1,0:T(8,128)(2,1)S(1)}, bf16[392,128]{1,0:T(8,128)(2,1)S(1)}, u32[]{:S(2)}, u32[]{:S(2)}) collective-permute-start(bf16[392,128]{1,0:T(8,128)(2,1)S(1)} %collective-permute-done.8.refs_9_), channel_id=1, source_target_pairs={{0,1},{1,0},{2,3},{3,2},{4,5},{5,4},{6,7},{7,6},{8,9},{9,8},{10,11... | collective-permute-start | bytes 301064 | tf_op jit(solution)/shard_map/ppermute | solution.py:488
  29.7 4.6 %collective-permute-start.14 = (bf16[200,128]{1,0:T(8,128)(2,1)S(1)}, bf16[200,128]{1,0:T(8,128)(2,1)S(1)}, u32[]{:S(2)}, u32[]{:S(2)}) collective-permute-start(bf16[200,128]{1,0:T(8,128)(2,1)S(1)} %collective-permute-done.12.refs_13_), channel_id=1, source_target_pairs={{0,2},{1,3},{2,0},{3,1},{4,6},{5,7},{6,4},{7,5},{8,10},{9,11},{10,... | collective-permute-start | bytes 153608 | tf_op jit(solution)/shard_map/ppermute | solution.py:488
  32.8 1.7 %collective-permute-start.13 = (bf16[200,128]{1,0:T(8,128)(2,1)S(1)}, bf16[200,128]{1,0:T(8,128)(2,1)S(1)}, u32[]{:S(2)}, u32[]{:S(2)}) collective-permute-start(bf16[200,128]{1,0:T(8,128)(2,1)S(1)} %collective-permute-done.12.refs_13_), channel_id=1, source_target_pairs={{0,1},{1,0},{2,3},{3,2},{4,5},{5,4},{6,7},{7,6},{8,9},{9,8},{10,11... | collective-permute-start | bytes 153608 | tf_op jit(solution)/shard_map/ppermute | solution.py:488
  33.6 2.6 %collective-permute-start.7 = (bf16[400,128]{1,0:T(8,128)(2,1)S(1)}, bf16[400,128]{1,0:T(8,128)(2,1)S(1)}, u32[]{:S(2)}, u32[]{:S(2)}) collective-permute-start(bf16[400,128]{1,0:T(8,128)(2,1)S(1)} %collective-permute-done.6.refs_6_), channel_id=1, source_target_pairs={{0,1},{1,0},{2,3},{3,2},{4,5},{5,4},{6,7},{7,6},{8,9},{9,8},{10,11... | collective-permute-start | bytes 307208 | tf_op jit(solution)/shard_map/ppermute | solution.py:488
  34.4 1.3 %collective-permute-start.11 = (bf16[392,128]{1,0:T(8,128)(2,1)S(1)}, bf16[392,128]{1,0:T(8,128)(2,1)S(1)}, u32[]{:S(2)}, u32[]{:S(2)}) collective-permute-start(bf16[392,128]{1,0:T(8,128)(2,1)S(1)} %collective-permute-done.10.refs_11_), channel_id=1, source_target_pairs={{0,1},{1,0},{2,3},{3,2},{4,5},{5,4},{6,7},{7,6},{8,9},{9,8},{10,11... | collective-permute-start | bytes 301064 | tf_op jit(solution)/shard_map/ppermute | solution.py:488
  34.4 1.4 %collective-permute-start.17 = (bf16[392,128]{1,0:T(8,128)(2,1)S(1)}, bf16[392,128]{1,0:T(8,128)(2,1)S(1)}, u32[]{:S(2)}, u32[]{:S(2)}) collective-permute-start(bf16[392,128]{1,0:T(8,128)(2,1)S(1)} %collective-permute-done.16.refs_17_), channel_id=1, source_target_pairs={{0,1},{1,0},{2,3},{3,2},{4,5},{5,4},{6,7},{7,6},{8,9},{9,8},{10,11... | collective-permute-start | bytes 301064 | tf_op jit(solution)/shard_map/ppermute | solution.py:488
  34.9 1.3 %collective-permute-start.19 = (bf16[392,128]{1,0:T(8,128)(2,1)S(1)}, bf16[392,128]{1,0:T(8,128)(2,1)S(1)}, u32[]{:S(2)}, u32[]{:S(2)}) collective-permute-start(bf16[392,128]{1,0:T(8,128)(2,1)S(1)} %collective-permute-done.18.refs_19_), channel_id=1, source_target_pairs={{0,1},{1,0},{2,3},{3,2},{4,5},{5,4},{6,7},{7,6},{8,9},{9,8},{10,11... | collective-permute-start | bytes 301064 | tf_op jit(solution)/shard_map/ppermute | solution.py:488

commit v3 on v2

--- a/solution.py
+++ b/solution.py
@@ -219,6 +219,10 @@
     )(*[in_vmem(value) for value in [info, *pieces]])
 
 
+def top_of(tile):
+    return jnp.max(jnp.max(tile, axis=1, keepdims=True), axis=0, keepdims=True)
+
+
 def describe_slots(row, duo, offsets, sides, far_side, group, offset_total):
     found = []
     for a in range(2):
@@ -231,8 +235,8 @@
         own_side = sides[0]
         for j in range(1, offset_total):
             own_side = jnp.where(k == j, sides[j], own_side)
-        own_source = jnp.where(side == 0, own_side == 0, far)
-        found.append((side, k, valid, own_source))
+        sign = jnp.where(side == 0, 1.0 - 2.0 * own_side.astype(jnp.float32), 2.0 * far - 1.0)
+        found.append((side, k, valid, jnp.max(sign) > 0.0, sign))
     return found
 
 
@@ -247,7 +251,7 @@
 
             def put(target, part, block, value):
                 rows = pl.ds(block * BLOCK_CH + top, count)
-                target[2 * seg + part, rows] = value.astype(jnp.bfloat16)
+                target[seg][part, rows] = value.astype(jnp.bfloat16)
 
             real, imag = ref[:count].astype(jnp.float32), ref[count : 2 * count].astype(jnp.float32)
             for m in range(span):
@@ -256,17 +260,17 @@
                 put(left, 1, m, imag * c)
                 put(left, 0, span + m, imag * minus)
                 put(left, 1, span + m, real * s)
-            for a, (_, _, _, own_source) in enumerate(slot_list):
+            for a, (_, _, _, _, sign) in enumerate(slot_list):
                 start = pl.multiple_of((2 * duo + a + 1) * 2 * count, 2 * count)
                 real = ref[pl.ds(start, count)].astype(jnp.float32)
                 imag = ref[pl.ds(start + count, count)].astype(jnp.float32)
-                s = s_mid * jnp.where(own_source, 1.0, -1.0)
+                s = s_mid * sign
                 put(right, 0, a, real * c_mid - imag * s)
                 put(right, 1, a, imag * c_mid + real * s)
 
 
 def contract(left, right):
-    wide = lambda ref: jnp.concatenate([ref[a] for a in range(ref.shape[0])], axis=1)
+    wide = lambda refs: jnp.concatenate([ref[part] for ref in refs for part in range(2)], axis=1)
     return lax.dot_general(
         wide(left), wide(right), (((1,), (1,)), ((), ())), preferred_element_type=jnp.float32
     )
@@ -287,8 +291,8 @@
 
 def factor_scratch(segs, span):
     return [
-        pltpu.VMEM((2 * segs, 2 * span * BLOCK_CH, BINS), jnp.bfloat16),
-        pltpu.VMEM((2 * segs, 2 * BLOCK_CH, BINS), jnp.bfloat16),
+        [pltpu.VMEM((2, 2 * span * BLOCK_CH, BINS), jnp.bfloat16)] * segs,
+        [pltpu.VMEM((2, 2 * BLOCK_CH, BINS), jnp.bfloat16)] * segs,
     ]
 
 
@@ -309,7 +313,7 @@
         lane = lax.broadcasted_iota(jnp.int32, (FLAG_ROWS, BINS), 1)
 
         def far_side(other, k):
-            return jnp.max(jnp.where(lane == k, flags_ref[other].astype(jnp.float32), 0.0)) > 0.5
+            return top_of(jnp.where(lane == k, flags_ref[other].astype(jnp.float32), 0.0))
 
         found = describe_slots(row, duo, offsets, sides, far_side, group, offset_total)
 
@@ -330,7 +334,7 @@
         def _():
             total[...] += product
 
-        for a, (side, k, valid, own_source) in enumerate(found):
+        for a, (side, k, valid, own_source, _) in enumerate(found):
             for a_side, out_ref in enumerate((first_ref, second_ref)):
                 for turned in (False, True):
                     here = jnp.logical_and(valid, step == steps - 1)
@@ -415,7 +419,7 @@
             for (turn, _), parts in zip(turns, held):
                 piece = parts[0][flag_at(slots, len(parts)) :].astype(jnp.float32)
                 flags = jnp.where(row ^ turn == other, piece, flags)
-            return jnp.max(jnp.where(lane == k, flags, 0.0)) > 0.5
+            return top_of(jnp.where(lane == k, flags, 0.0))
 
         found = describe_slots(row, 0, offsets, sides, far_side, group, offset_total)
 
@@ -433,12 +437,10 @@
         def copy_to(out_hbm, a, k, lag):
             return pltpu.make_async_copy(result.at[a, lag], out_hbm.at[0, k, lag], sems.at[a, lag])
 
-        @pl.when(jnp.logical_or(found[0][2], found[1][2]))
-        def _():
-            fill_factors(held, found, 0, pair, tables, left, right)
-            total[...] = contract(left, right)
-
-        for a, (side, k, valid, own_source) in enumerate(found):
+        fill_factors(held, found, 0, pair, tables, left, right)
+        total[...] = contract(left, right)
+
+        for a, (side, k, valid, own_source, _) in enumerate(found):
             for turned in (False, True):
 
                 @pl.when(jnp.logical_and(valid, own_source != turned))
@@ -450,7 +452,7 @@
 
                     lag_values(total, a, span, turned, put)
 
-        for a, (side, k, valid, own_source) in enumerate(found):
+        for a, (side, k, valid, own_source, _) in enumerate(found):
 
             @pl.when(valid)
             def _():

time: 39.5 us -> 39.3 us (level)
  no operation moved by 1% of the time
where the time goes in v3:
time: 39.3 us; the launch traced here: 39.1 us
  starting transfers between devices  19.3 us (49%)
  waiting for transfers between devices  13.3 us (34%)
  Pallas kernels  5.82 us (15%)
  between operations  0.72 us (2%)
    ppermute x20, starting transfers between devices, swap(): lax.ppermute(value, axis, [(a, a ^ turn) for a in range(lax.axis_size(axi...  19.3 us
    ppermute x20, waiting for transfers between devices, swap(): lax.ppermute(value, axis, [(a, a ^ turn) for a in range(lax.axis_size(axi...  13.3 us
    pallas_call x1, Pallas kernels, correlate_turns(): pl.pallas_call(kernel, in_specs=[VMEM_SPEC] * (4 + len(operands)), out_sp...  2.92 us
    pallas_call x1, Pallas kernels, whiten(): pl.pallas_call(kernel, grid=(blocks // step_blocks,), in_specs=[pl.BlockS...  2.69 us
  transfers between devices with their start and end apart: 20, of which 9 were waited for; matrix products, arithmetic and copies ran while one was open for 0% of the time, Pallas kernels for 0%

profile of v3, /device:TPU:0, one launch (start us, length us, event | category | flops | bytes accessed | tf_op | source)
XLA Modules:
  0.0 39.1 jit_solution(14799984000411360112)
XLA Ops:
  0.7 2.7 %whiten.1 = (bf16[2,2,64,128]{3,2,1,0:T(8,128)(2,1)S(1)}, bf16[2,2,64,128]{3,2,1,0:T(8,128)(2,1)S(1)}, f32[8,128]{1,0:T(8,128)S(1)}) custom-call(s32[2]{0:T(128)} %offsets_hbm.1, s32[1,2]{1,0:T(1,128)} %side_hbm.1, bf16[256,2048]{1,0:T(8,128)(2,1)} %bitcast.1, bf16[2048,512]{1,0:T(8,128)(2,1)} %constant.8.clone.table_hbm), custom_call_target="tpu_custom_call" | custom-call | tf_op jit(solution)/shard_map/whiten/pallas_call | solution.py:108
  3.4 3.1 %collective-permute-start.1 = (bf16[2,2,64,128]{3,2,1,0:T(8,128)(2,1)S(1)}, bf16[2,2,64,128]{3,2,1,0:T(8,128)(2,1)S(1)}, u32[]{:S(2)}, u32[]{:S(2)}) collective-permute-start(bf16[2,2,64,128]{3,2,1,0:T(8,128)(2,1)S(1)} %get-tuple-element.16.refs_0_), channel_id=1, source_target_pairs={{0,2},{1,3},{2,0},{3,1},{4,6},{5,7},{6,4},{7,5},{8,10},{9,11},{10,... | collective-permute-start | bytes 196616 | tf_op jit(solution)/shard_map/ppermute | solution.py:490
  6.4 0.2 collective-permute-start
  6.6 2.1 %collective-permute-done.1.refs_2_ = bf16[2,2,64,128]{3,2,1,0:T(8,128)(2,1)S(1)} collective-permute-done((bf16[2,2,64,128]{3,2,1,0:T(8,128)(2,1)S(1)}, bf16[2,2,64,128]{3,2,1,0:T(8,128)(2,1)S(1)}, u32[]{:S(2)}, u32[]{:S(2)}) %collective-permute-start.1) | collective-permute-done | bytes 65568 | tf_op jit(solution)/shard_map/ppermute | solution.py:490
  8.7 1.9 %collective-permute-done.2.refs_3_ = bf16[2,2,64,128]{3,2,1,0:T(8,128)(2,1)S(1)} collective-permute-done((bf16[2,2,64,128]{3,2,1,0:T(8,128)(2,1)S(1)}, bf16[2,2,64,128]{3,2,1,0:T(8,128)(2,1)S(1)}, u32[]{:S(2)}, u32[]{:S(2)}) %collective-permute-start.2) | collective-permute-done | bytes 65568 | tf_op jit(solution)/shard_map/ppermute | solution.py:490
  10.6 0.2 pack.1
  10.8 3.7 %collective-permute-start.3 = (bf16[200,128]{1,0:T(8,128)(2,1)S(1)}, bf16[200,128]{1,0:T(8,128)(2,1)S(1)}, u32[]{:S(2)}, u32[]{:S(2)}) collective-permute-start(bf16[200,128]{1,0:T(8,128)(2,1)S(1)} %get-tuple-element.19), channel_id=1, source_target_pairs={{0,24},{4,28},{8,16},{12,20},{16,8},{20,12},{24,0},{28,4},{1,25},{... | collective-permute-start | bytes 153608 | tf_op jit(solution)/shard_map/ppermute | solution.py:490
  14.4 1.5 %collective-permute-start.8 = (bf16[392,128]{1,0:T(8,128)(2,1)S(1)}, bf16[392,128]{1,0:T(8,128)(2,1)S(1)}, u32[]{:S(2)}, u32[]{:S(2)}) collective-permute-start(bf16[392,128]{1,0:T(8,128)(2,1)S(1)} %get-tuple-element.23), channel_id=1, source_target_pairs={{0,4},{4,0},{8,12},{12,8},{16,20},{20,16},{24,28},{28,24},{1,5},{5... | collective-permute-start | bytes 301064 | tf_op jit(solution)/shard_map/ppermute | solution.py:490
  15.9 0.7 %collective-permute-start.10 = (bf16[392,128]{1,0:T(8,128)(2,1)S(1)}, bf16[392,128]{1,0:T(8,128)(2,1)S(1)}, u32[]{:S(2)}, u32[]{:S(2)}) collective-permute-start(bf16[392,128]{1,0:T(8,128)(2,1)S(1)} %get-tuple-element.24), channel_id=1, source_target_pairs={{0,12},{4,8},{8,4},{12,0},{16,28},{20,24},{24,20},{28,16},{1,13},{... | collective-permute-start | bytes 301064 | tf_op jit(solution)/shard_map/ppermute | solution.py:490
  16.7 4.5 %collective-permute-start.16 = (bf16[392,128]{1,0:T(8,128)(2,1)S(1)}, bf16[392,128]{1,0:T(8,128)(2,1)S(1)}, u32[]{:S(2)}, u32[]{:S(2)}) collective-permute-start(bf16[392,128]{1,0:T(8,128)(2,1)S(1)} %get-tuple-element.26), channel_id=1, source_target_pairs={{0,28},{4,24},{8,20},{12,16},{16,12},{20,8},{24,4},{28,0},{1,29},{... | collective-permute-start | bytes 301064 | tf_op jit(solution)/shard_map/ppermute | solution.py:490
  21.2 0.9 %collective-permute-start.18 = (bf16[392,128]{1,0:T(8,128)(2,1)S(1)}, bf16[392,128]{1,0:T(8,128)(2,1)S(1)}, u32[]{:S(2)}, u32[]{:S(2)}) collective-permute-start(bf16[392,128]{1,0:T(8,128)(2,1)S(1)} %get-tuple-element.27), channel_id=1, source_target_pairs={{0,8},{4,12},{8,0},{12,4},{16,24},{20,28},{24,16},{28,20},{1,9},{5... | collective-permute-start | bytes 301064 | tf_op jit(solution)/shard_map/ppermute | solution.py:490
  22.1 5.4 %collective-permute-done.12.refs_13_ = bf16[200,128]{1,0:T(8,128)(2,1)S(1)} collective-permute-done((bf16[200,128]{1,0:T(8,128)(2,1)S(1)}, bf16[200,128]{1,0:T(8,128)(2,1)S(1)}, u32[]{:S(2)}, u32[]{:S(2)}) %collective-permute-start.12) | collective-permute-done | bytes 51232 | tf_op jit(solution)/shard_map/ppermute | solution.py:490
  27.5 1.2 %collective-permute-start.6 = (bf16[400,128]{1,0:T(8,128)(2,1)S(1)}, bf16[400,128]{1,0:T(8,128)(2,1)S(1)}, u32[]{:S(2)}, u32[]{:S(2)}) collective-permute-start(bf16[400,128]{1,0:T(8,128)(2,1)S(1)} %get-tuple-element.22), channel_id=1, source_target_pairs={{0,2},{1,3},{2,0},{3,1},{4,6},{5,7},{6,4},{7,5},{8,10},{9,11},{10,... | collective-permute-start | bytes 307208 | tf_op jit(solution)/shard_map/ppermute | solution.py:490
  28.7 0.9 %collective-permute-start.5 = (bf16[792,128]{1,0:T(8,128)(2,1)S(1)}, bf16[792,128]{1,0:T(8,128)(2,1)S(1)}, u32[]{:S(2)}, u32[]{:S(2)}) collective-permute-start(bf16[792,128]{1,0:T(8,128)(2,1)S(1)} %get-tuple-element.21), channel_id=1, source_target_pairs={{0,1},{1,0},{2,3},{3,2},{4,5},{5,4},{6,7},{7,6},{8,9},{9,8},{10,11... | collective-permute-start | bytes 608264 | tf_op jit(solution)/shard_map/ppermute | solution.py:490
  29.7 1.2 %collective-permute-start.14 = (bf16[200,128]{1,0:T(8,128)(2,1)S(1)}, bf16[200,128]{1,0:T(8,128)(2,1)S(1)}, u32[]{:S(2)}, u32[]{:S(2)}) collective-permute-start(bf16[200,128]{1,0:T(8,128)(2,1)S(1)} %collective-permute-done.12.refs_13_), channel_id=1, source_target_pairs={{0,2},{1,3},{2,0},{3,1},{4,6},{5,7},{6,4},{7,5},{8,10},{9,11},{10,... | collective-permute-start | bytes 153608 | tf_op jit(solution)/shard_map/ppermute | solution.py:490
  30.9 1.9 %collective-permute-done.15.refs_16_ = bf16[200,128]{1,0:T(8,128)(2,1)S(1)} collective-permute-done((bf16[200,128]{1,0:T(8,128)(2,1)S(1)}, bf16[200,128]{1,0:T(8,128)(2,1)S(1)}, u32[]{:S(2)}, u32[]{:S(2)}) %collective-permute-start.15) | collective-permute-done | bytes 51232 | tf_op jit(solution)/shard_map/ppermute | solution.py:490
  32.8 0.8 %collective-permute-start.13 = (bf16[200,128]{1,0:T(8,128)(2,1)S(1)}, bf16[200,128]{1,0:T(8,128)(2,1)S(1)}, u32[]{:S(2)}, u32[]{:S(2)}) collective-permute-start(bf16[200,128]{1,0:T(8,128)(2,1)S(1)} %collective-permute-done.12.refs_13_), channel_id=1, source_target_pairs={{0,1},{1,0},{2,3},{3,2},{4,5},{5,4},{6,7},{7,6},{8,9},{9,8},{10,11... | collective-permute-start | bytes 153608 | tf_op jit(solution)/shard_map/ppermute | solution.py:490
  33.6 0.8 %collective-permute-done.14.refs_15_ = bf16[200,128]{1,0:T(8,128)(2,1)S(1)} collective-permute-done((bf16[200,128]{1,0:T(8,128)(2,1)S(1)}, bf16[200,128]{1,0:T(8,128)(2,1)S(1)}, u32[]{:S(2)}, u32[]{:S(2)}) %collective-permute-start.14) | collective-permute-done | bytes 51232 | tf_op jit(solution)/shard_map/ppermute | solution.py:490
  34.4 0.1 collective-permute-done.13.refs_14_
  34.4 0.4 %collective-permute-start.17 = (bf16[392,128]{1,0:T(8,128)(2,1)S(1)}, bf16[392,128]{1,0:T(8,128)(2,1)S(1)}, u32[]{:S(2)}, u32[]{:S(2)}) collective-permute-start(bf16[392,128]{1,0:T(8,128)(2,1)S(1)} %collective-permute-done.16.refs_17_), channel_id=1, source_target_pairs={{0,1},{1,0},{2,3},{3,2},{4,5},{5,4},{6,7},{7,6},{8,9},{9,8},{10,11... | collective-permute-start | bytes 301064 | tf_op jit(solution)/shard_map/ppermute | solution.py:490
  34.9 0.7 %collective-permute-done.11.refs_12_ = bf16[392,128]{1,0:T(8,128)(2,1)S(1)} collective-permute-done((bf16[392,128]{1,0:T(8,128)(2,1)S(1)}, bf16[392,128]{1,0:T(8,128)(2,1)S(1)}, u32[]{:S(2)}, u32[]{:S(2)}) %collective-permute-start.11) | collective-permute-done | bytes 100384 | tf_op jit(solution)/shard_map/ppermute | solution.py:490
  35.7 0.2 collective-permute-done.17.refs_18_
  35.8 0.4 collective-permute-done.19.refs_20_
  36.2 2.9 %correlate.1 = (bf16[1,2,8,128,128]{4,3,2,1,0:T(8,128)(2,1)}, bf16[1,2,8,128,128]{4,3,2,1,0:T(8,128)(2,1)}) custom-call(f32[8,128]{1,0:T(8,128)S(1)} %get-tuple-element.15.info_ref, f32[4,128]{1,0:T(4,128)S(1)} %copy-done.2, f32[4,128]{1,0:T(4,128)S(1)} %copy-done.1, f32[3,4,128]{2,1,0:T(4,128)S(1)} %copy-done, ...), custom_call_target="tpu_custom_call" | custom-call | tf_op jit(solution)/shard_map/correlate/pallas_call | solution.py:467
  (26 shorter events, 0.2 us)
Async XLA Ops:
  0.6 35.6 %copy-start = (f32[3,4,128]{2,1,0:T(4,128)S(1)}, f32[3,4,128]{2,1,0:T(4,128)}, u32[]{:S(2)}) copy-start(f32[3,4,128]{2,1,0:T(4,128)} %constant.11.clone.refs_2_) | copy-start | bytes 18436
  0.6 35.5 %copy-start.1 = (f32[4,128]{1,0:T(4,128)S(1)}, f32[4,128]{1,0:T(4,128)}, u32[]{:S(2)}) copy-start(f32[4,128]{1,0:T(4,128)} %constant.10.clone.refs_1_) | copy-start | bytes 6148
  0.7 35.5 %copy-start.2 = (f32[4,128]{1,0:T(4,128)S(1)}, f32[4,128]{1,0:T(4,128)}, u32[]{:S(2)}) copy-start(f32[4,128]{1,0:T(4,128)} %constant.9.clone.refs_0_) | copy-start | bytes 6148
  3.4 5.3 %collective-permute-start.1 = (bf16[2,2,64,128]{3,2,1,0:T(8,128)(2,1)S(1)}, bf16[2,2,64,128]{3,2,1,0:T(8,128)(2,1)S(1)}, u32[]{:S(2)}, u32[]{:S(2)}) collective-permute-start(bf16[2,2,64,128]{3,2,1,0:T(8,128)(2,1)S(1)} %get-tuple-element.16.refs_0_), channel_id=1, source_target_pairs={{0,2},{1,3},{2,0},{3,1},{4,6},{5,7},{6,4},{7,5},{8,10},{9,11},{10,... | collective-permute-start | bytes 196616 | tf_op jit(solution)/shard_map/ppermute | solution.py:490
  6.4 4.1 %collective-permute-start.2 = (bf16[2,2,64,128]{3,2,1,0:T(8,128)(2,1)S(1)}, bf16[2,2,64,128]{3,2,1,0:T(8,128)(2,1)S(1)}, u32[]{:S(2)}, u32[]{:S(2)}) collective-permute-start(bf16[2,2,64,128]{3,2,1,0:T(8,128)(2,1)S(1)} %get-tuple-element.17), channel_id=1, source_target_pairs={{0,3},{1,2},{2,1},{3,0},{4,7},{5,6},{6,5},{7,4},{8,11},{9,10},{10,... | collective-permute-start | bytes 196616 | tf_op jit(solution)/shard_map/ppermute | solution.py:490
  6.4 4.1 %collective-permute-start = (bf16[2,2,64,128]{3,2,1,0:T(8,128)(2,1)S(1)}, bf16[2,2,64,128]{3,2,1,0:T(8,128)(2,1)S(1)}, u32[]{:S(2)}, u32[]{:S(2)}) collective-permute-start(bf16[2,2,64,128]{3,2,1,0:T(8,128)(2,1)S(1)} %get-tuple-element.17), channel_id=1, source_target_pairs={{0,1},{1,0},{2,3},{3,2},{4,5},{5,4},{6,7},{7,6},{8,9},{9,8},{10,11... | collective-permute-start | bytes 196616 | tf_op jit(solution)/shard_map/ppermute | solution.py:490
  10.8 10.5 %collective-permute-start.3 = (bf16[200,128]{1,0:T(8,128)(2,1)S(1)}, bf16[200,128]{1,0:T(8,128)(2,1)S(1)}, u32[]{:S(2)}, u32[]{:S(2)}) collective-permute-start(bf16[200,128]{1,0:T(8,128)(2,1)S(1)} %get-tuple-element.19), channel_id=1, source_target_pairs={{0,24},{4,28},{8,16},{12,20},{16,8},{20,12},{24,0},{28,4},{1,25},{... | collective-permute-start | bytes 153608 | tf_op jit(solution)/shard_map/ppermute | solution.py:490
  14.4 6.8 %collective-permute-start.4 = (bf16[200,128]{1,0:T(8,128)(2,1)S(1)}, bf16[200,128]{1,0:T(8,128)(2,1)S(1)}, u32[]{:S(2)}, u32[]{:S(2)}) collective-permute-start(bf16[200,128]{1,0:T(8,128)(2,1)S(1)} %get-tuple-element.20), channel_id=1, source_target_pairs={{0,16},{4,20},{8,24},{12,28},{16,0},{20,4},{24,8},{28,12},{1,17},{... | collective-permute-start | bytes 153608 | tf_op jit(solution)/shard_map/ppermute | solution.py:490
  14.4 14.2 %collective-permute-start.8 = (bf16[392,128]{1,0:T(8,128)(2,1)S(1)}, bf16[392,128]{1,0:T(8,128)(2,1)S(1)}, u32[]{:S(2)}, u32[]{:S(2)}) collective-permute-start(bf16[392,128]{1,0:T(8,128)(2,1)S(1)} %get-tuple-element.23), channel_id=1, source_target_pairs={{0,4},{4,0},{8,12},{12,8},{16,20},{20,16},{24,28},{28,24},{1,5},{5... | collective-permute-start | bytes 301064 | tf_op jit(solution)/shard_map/ppermute | solution.py:490
  15.9 12.8 %collective-permute-start.10 = (bf16[392,128]{1,0:T(8,128)(2,1)S(1)}, bf16[392,128]{1,0:T(8,128)(2,1)S(1)}, u32[]{:S(2)}, u32[]{:S(2)}) collective-permute-start(bf16[392,128]{1,0:T(8,128)(2,1)S(1)} %get-tuple-element.24), channel_id=1, source_target_pairs={{0,12},{4,8},{8,4},{12,0},{16,28},{20,24},{24,20},{28,16},{1,13},{... | collective-permute-start | bytes 301064 | tf_op jit(solution)/shard_map/ppermute | solution.py:490
  16.7 13.0 %collective-permute-start.16 = (bf16[392,128]{1,0:T(8,128)(2,1)S(1)}, bf16[392,128]{1,0:T(8,128)(2,1)S(1)}, u32[]{:S(2)}, u32[]{:S(2)}) collective-permute-start(bf16[392,128]{1,0:T(8,128)(2,1)S(1)} %get-tuple-element.26), channel_id=1, source_target_pairs={{0,28},{4,24},{8,20},{12,16},{16,12},{20,8},{24,4},{28,0},{1,29},{... | collective-permute-start | bytes 301064 | tf_op jit(solution)/shard_map/ppermute | solution.py:490
  21.2 6.3 %collective-permute-start.12 = (bf16[200,128]{1,0:T(8,128)(2,1)S(1)}, bf16[200,128]{1,0:T(8,128)(2,1)S(1)}, u32[]{:S(2)}, u32[]{:S(2)}) collective-permute-start(bf16[200,128]{1,0:T(8,128)(2,1)S(1)} %get-tuple-element.25), channel_id=1, source_target_pairs={{0,20},{4,16},{8,28},{12,24},{16,4},{20,0},{24,12},{28,8},{1,21},{... | collective-permute-start | bytes 153608 | tf_op jit(solution)/shard_map/ppermute | solution.py:490
  21.2 8.5 %collective-permute-start.18 = (bf16[392,128]{1,0:T(8,128)(2,1)S(1)}, bf16[392,128]{1,0:T(8,128)(2,1)S(1)}, u32[]{:S(2)}, u32[]{:S(2)}) collective-permute-start(bf16[392,128]{1,0:T(8,128)(2,1)S(1)} %get-tuple-element.27), channel_id=1, source_target_pairs={{0,8},{4,12},{8,0},{12,4},{16,24},{20,28},{24,16},{28,20},{1,9},{5... | collective-permute-start | bytes 301064 | tf_op jit(solution)/shard_map/ppermute | solution.py:490
  27.5 6.1 %collective-permute-start.6 = (bf16[400,128]{1,0:T(8,128)(2,1)S(1)}, bf16[400,128]{1,0:T(8,128)(2,1)S(1)}, u32[]{:S(2)}, u32[]{:S(2)}) collective-permute-start(bf16[400,128]{1,0:T(8,128)(2,1)S(1)} %get-tuple-element.22), channel_id=1, source_target_pairs={{0,2},{1,3},{2,0},{3,1},{4,6},{5,7},{6,4},{7,5},{8,10},{9,11},{10,... | collective-permute-start | bytes 307208 | tf_op jit(solution)/shard_map/ppermute | solution.py:490
  28.7 4.1 %collective-permute-start.15 = (bf16[200,128]{1,0:T(8,128)(2,1)S(1)}, bf16[200,128]{1,0:T(8,128)(2,1)S(1)}, u32[]{:S(2)}, u32[]{:S(2)}) collective-permute-start(bf16[200,128]{1,0:T(8,128)(2,1)S(1)} %collective-permute-done.12.refs_13_), channel_id=1, source_target_pairs={{0,3},{1,2},{2,1},{3,0},{4,7},{5,6},{6,5},{7,4},{8,11},{9,10},{10,... | collective-permute-start | bytes 153608 | tf_op jit(solution)/shard_map/ppermute | solution.py:490
  28.7 7.5 %collective-permute-start.5 = (bf16[792,128]{1,0:T(8,128)(2,1)S(1)}, bf16[792,128]{1,0:T(8,128)(2,1)S(1)}, u32[]{:S(2)}, u32[]{:S(2)}) collective-permute-start(bf16[792,128]{1,0:T(8,128)(2,1)S(1)} %get-tuple-element.21), channel_id=1, source_target_pairs={{0,1},{1,0},{2,3},{3,2},{4,5},{5,4},{6,7},{7,6},{8,9},{9,8},{10,11... | collective-permute-start | bytes 608264 | tf_op jit(solution)/shard_map/ppermute | solution.py:490
  29.7 5.2 %collective-permute-start.9 = (bf16[392,128]{1,0:T(8,128)(2,1)S(1)}, bf16[392,128]{1,0:T(8,128)(2,1)S(1)}, u32[]{:S(2)}, u32[]{:S(2)}) collective-permute-start(bf16[392,128]{1,0:T(8,128)(2,1)S(1)} %collective-permute-done.8.refs_9_), channel_id=1, source_target_pairs={{0,1},{1,0},{2,3},{3,2},{4,5},{5,4},{6,7},{7,6},{8,9},{9,8},{10,11... | collective-permute-start | bytes 301064 | tf_op jit(solution)/shard_map/ppermute | solution.py:490
  29.7 4.6 %collective-permute-start.14 = (bf16[200,128]{1,0:T(8,128)(2,1)S(1)}, bf16[200,128]{1,0:T(8,128)(2,1)S(1)}, u32[]{:S(2)}, u32[]{:S(2)}) collective-permute-start(bf16[200,128]{1,0:T(8,128)(2,1)S(1)} %collective-permute-done.12.refs_13_), channel_id=1, source_target_pairs={{0,2},{1,3},{2,0},{3,1},{4,6},{5,7},{6,4},{7,5},{8,10},{9,11},{10,... | collective-permute-start | bytes 153608 | tf_op jit(solution)/shard_map/ppermute | solution.py:490
  32.8 1.7 %collective-permute-start.13 = (bf16[200,128]{1,0:T(8,128)(2,1)S(1)}, bf16[200,128]{1,0:T(8,128)(2,1)S(1)}, u32[]{:S(2)}, u32[]{:S(2)}) collective-permute-start(bf16[200,128]{1,0:T(8,128)(2,1)S(1)} %collective-permute-done.12.refs_13_), channel_id=1, source_target_pairs={{0,1},{1,0},{2,3},{3,2},{4,5},{5,4},{6,7},{7,6},{8,9},{9,8},{10,11... | collective-permute-start | bytes 153608 | tf_op jit(solution)/shard_map/ppermute | solution.py:490
  33.6 2.6 %collective-permute-start.7 = (bf16[400,128]{1,0:T(8,128)(2,1)S(1)}, bf16[400,128]{1,0:T(8,128)(2,1)S(1)}, u32[]{:S(2)}, u32[]{:S(2)}) collective-permute-start(bf16[400,128]{1,0:T(8,128)(2,1)S(1)} %collective-permute-done.6.refs_6_), channel_id=1, source_target_pairs={{0,1},{1,0},{2,3},{3,2},{4,5},{5,4},{6,7},{7,6},{8,9},{9,8},{10,11... | collective-permute-start | bytes 307208 | tf_op jit(solution)/shard_map/ppermute | solution.py:490
  34.4 1.3 %collective-permute-start.11 = (bf16[392,128]{1,0:T(8,128)(2,1)S(1)}, bf16[392,128]{1,0:T(8,128)(2,1)S(1)}, u32[]{:S(2)}, u32[]{:S(2)}) collective-permute-start(bf16[392,128]{1,0:T(8,128)(2,1)S(1)} %collective-permute-done.10.refs_11_), channel_id=1, source_target_pairs={{0,1},{1,0},{2,3},{3,2},{4,5},{5,4},{6,7},{7,6},{8,9},{9,8},{10,11... | collective-permute-start | bytes 301064 | tf_op jit(solution)/shard_map/ppermute | solution.py:490
  34.4 1.4 %collective-permute-start.17 = (bf16[392,128]{1,0:T(8,128)(2,1)S(1)}, bf16[392,128]{1,0:T(8,128)(2,1)S(1)}, u32[]{:S(2)}, u32[]{:S(2)}) collective-permute-start(bf16[392,128]{1,0:T(8,128)(2,1)S(1)} %collective-permute-done.16.refs_17_), channel_id=1, source_target_pairs={{0,1},{1,0},{2,3},{3,2},{4,5},{5,4},{6,7},{7,6},{8,9},{9,8},{10,11... | collective-permute-start | bytes 301064 | tf_op jit(solution)/shard_map/ppermute | solution.py:490
  34.9 1.3 %collective-permute-start.19 = (bf16[392,128]{1,0:T(8,128)(2,1)S(1)}, bf16[392,128]{1,0:T(8,128)(2,1)S(1)}, u32[]{:S(2)}, u32[]{:S(2)}) collective-permute-start(bf16[392,128]{1,0:T(8,128)(2,1)S(1)} %collective-permute-done.18.refs_19_), channel_id=1, source_target_pairs={{0,1},{1,0},{2,3},{3,2},{4,5},{5,4},{6,7},{7,6},{8,9},{9,8},{10,11... | collective-permute-start | bytes 301064 | tf_op jit(solution)/shard_map/ppermute | solution.py:490
